TPU v7x, 32 devices: a whole 2x2x4 slice. The times are simulated.
32 devices in a mesh: shard: 4 (over z), ctx: 4 (over y, core), tp: 2 (over x).
Axes of the slice: x: 2, y: 2, z: 4, core: 2. Of those that a mesh axis runs over, the one named last changes fastest.
Arguments:
- block_input: float32 [2048, 640], P(('shard', 'ctx')), may hold values from -6 to 6
- out_cotangent: float32 [2048, 640], P(('shard', 'ctx')), may hold values from -6 to 6
- seq_lengths: int32 [4, 4], P('shard'), may hold values from 1 to 256, 512 in all within a row
- q_weight: bfloat16 [640, 1024], P('shard', 'tp'), may hold values from -0.25 to 0.25
- k_weight: bfloat16 [640, 256], P('shard'), may hold values from -0.25 to 0.25
- v_weight: bfloat16 [640, 256], P('shard'), may hold values from -0.25 to 0.25
- o_weight: bfloat16 [640, 1024], P('shard', 'tp'), may hold values from -0.1875 to 0.1875
- gate_weight: bfloat16 [640, 2048], P('shard', 'tp'), may hold values from -0.25 to 0.25
- up_weight: bfloat16 [640, 2048], P('shard', 'tp'), may hold values from -0.25 to 0.25
- down_weight: bfloat16 [640, 2048], P('shard', 'tp'), may hold values from -0.125 to 0.125
- attn_in_gain: bfloat16 [640], P('shard'), may hold values from 0.25 to 1.75
- attn_out_gain: bfloat16 [640], P('shard'), may hold values from 0.25 to 1.75
- ffn_in_gain: bfloat16 [640], P('shard'), may hold values from 0.25 to 1.75
- ffn_out_gain: bfloat16 [640], P('shard'), may hold values from 0.25 to 1.75
- query_gain: bfloat16 [256], P('shard'), may hold values from 0.25 to 1.75
- key_gain: bfloat16 [256], P('shard'), may hold values from 0.25 to 1.75
Outputs:
- block_output: float32 [2048, 640], P(('shard', 'ctx'))
- input_grad: float32 [2048, 640], P(('shard', 'ctx'))
- q_weight_grad: float32 [640, 1024], P('shard', 'tp')
- k_weight_grad: float32 [640, 256], P('shard')
- v_weight_grad: float32 [640, 256], P('shard')
- o_weight_grad: float32 [640, 1024], P('shard', 'tp')
- gate_weight_grad: float32 [640, 2048], P('shard', 'tp')
- up_weight_grad: float32 [640, 2048], P('shard', 'tp')
- down_weight_grad: float32 [640, 2048], P('shard', 'tp')
- attn_in_gain_grad: float32 [640], P('shard')
- attn_out_gain_grad: float32 [640], P('shard')
- ffn_in_gain_grad: float32 [640], P('shard')
- ffn_out_gain_grad: float32 [640], P('shard')
- query_gain_grad: float32 [256], P('shard')
- key_gain_grad: float32 [256], P('shard')
Inputs may be any that keep to these rules, and one draw needn't show every extreme that they name: Row b of seq_lengths lists the 4 sequences packed into row b in order; they sum to 512, and the longest of every row has exactly 256 tokens.
All inputs are finite; a program needn't handle non-finite values.
Results may differ from a plain program's by a relative error of at most 0.015.
Values may be sent and summed in bfloat16 or wider, within the bound.
A program may use at most 64 MiB of HBM per device.

v0:
```python
import jax
import jax.numpy as jnp
from jax import lax
from jax.sharding import PartitionSpec as P

HD = 256


eps = 1e-06
rope_base = 1000000.0


def dot_plain(left, right):
    return jnp.dot(left, right, preferred_element_type=jnp.float32)


def dot_last(left, right):
    return lax.dot_general(
        left, right, (((1,), (1,)), ((), ())), preferred_element_type=jnp.float32
    )


def dot_first(left, right):
    return lax.dot_general(
        left, right, (((0,), (0,)), ((), ())), preferred_element_type=jnp.float32
    )


def norm_parts(value):
    scale = lax.rsqrt(jnp.mean(value * value, axis=-1, keepdims=True) + eps)
    return (value * scale, scale)


def norm_back(dnormed, unit, scale):
    return scale * (dnormed - unit * jnp.mean(dnormed * unit, axis=-1, keepdims=True))


def rope_tables(position):
    freq = rope_base ** (-jnp.arange(HD // 2).astype(jnp.float32) * (2.0 / HD))
    angle = position.astype(jnp.float32)[:, None] * freq[None, :]
    return (jnp.cos(angle), jnp.sin(angle))


def rotate(value, cosine, sine):
    half = value.shape[-1] // 2
    first, second = (value[..., :half], value[..., half:])
    return jnp.concatenate(
        [first * cosine - second * sine, second * cosine + first * sine], axis=-1
    )


def unrotate(value, cosine, sine):
    half = value.shape[-1] // 2
    first, second = (value[..., :half], value[..., half:])
    return jnp.concatenate(
        [first * cosine + second * sine, second * cosine - first * sine], axis=-1
    )


def layout(lengths, count):
    index = jnp.arange(count)
    ends = jnp.cumsum(lengths)
    after = (index[:, None] >= ends[None, :]).astype(jnp.int32)
    segment = jnp.sum(after, axis=1)
    position = index - jnp.sum(after * lengths[None, :], axis=1)
    return (segment, position)


def gelu_tanh(value):
    return jax.nn.gelu(value, approximate=True)


def masked_scores(query_head, key_block, mask, scaling):
    raw = dot_last(query_head, key_block) * scaling
    return jnp.where(mask, raw, -1e30)


def per_device(
    block_input,
    out_cotangent,
    seq_lengths,
    q_weight,
    k_weight,
    v_weight,
    o_weight,
    gate_weight,
    up_weight,
    down_weight,
    attn_in_gain,
    attn_out_gain,
    ffn_in_gain,
    ffn_out_gain,
    query_gain,
    key_gain,
):
    tokens = block_input.shape[0]
    width = block_input.shape[1]
    n_ctx = lax.axis_size("ctx")
    n_tp = lax.axis_size("tp")
    row_len = tokens * n_ctx
    piece = tokens // n_tp
    my_start = lax.axis_index("ctx") * tokens
    my_sub = lax.axis_index("tp") * piece
    scaling = HD ** (-0.5)
    segment, position = layout(seq_lengths[0], row_len)
    key_index = jnp.arange(row_len)
    query_index = my_start + jnp.arange(tokens)
    query_seg = lax.dynamic_slice_in_dim(segment, my_start, tokens)
    allowed = (query_seg[:, None] == segment[None, :]) & (
        key_index[None, :] <= query_index[:, None]
    )
    cosine, sine = rope_tables(lax.dynamic_slice_in_dim(position, my_start, tokens))
    gathered = (
        lax.all_gather(q_weight, "shard", axis=0, tiled=True),
        lax.all_gather(k_weight, "shard", axis=0, tiled=True),
        lax.all_gather(v_weight, "shard", axis=0, tiled=True),
        lax.all_gather(o_weight, "shard", axis=0, tiled=True),
        lax.all_gather(gate_weight, "shard", axis=0, tiled=True),
        lax.all_gather(up_weight, "shard", axis=0, tiled=True),
        lax.all_gather(down_weight, "shard", axis=0, tiled=True),
        lax.all_gather(attn_in_gain, "shard", axis=0, tiled=True),
        lax.all_gather(attn_out_gain, "shard", axis=0, tiled=True),
        lax.all_gather(ffn_in_gain, "shard", axis=0, tiled=True),
        lax.all_gather(ffn_out_gain, "shard", axis=0, tiled=True),
        lax.all_gather(query_gain, "shard", axis=0, tiled=True),
        lax.all_gather(key_gain, "shard", axis=0, tiled=True),
    )
    qw, kw, vw, ow, gw, uw, dw = gathered[:7]
    g_ai, g_ao, g_fi, g_fo, g_q, g_k = [item.astype(jnp.float32) for item in gathered[7:]]
    local_heads = qw.shape[1] // HD
    unit1, r1 = norm_parts(block_input)
    xn1 = (unit1 * g_ai).astype(jnp.bfloat16)
    qp = dot_plain(xn1, qw).reshape(tokens, local_heads, HD)
    qunit, rq = norm_parts(qp)
    queries = rotate(qunit * g_q, cosine[:, None, :], sine[:, None, :]).astype(jnp.bfloat16)
    kp = dot_plain(xn1, kw)
    kunit, rk = norm_parts(kp)
    keys = rotate(kunit * g_k, cosine, sine).astype(jnp.bfloat16)
    values = dot_plain(xn1, vw).astype(jnp.bfloat16)
    row_keys, row_values = (
        lax.all_gather(keys, "ctx", axis=0, tiled=True),
        lax.all_gather(values, "ctx", axis=0, tiled=True),
    )
    head_outs = []
    lses = []
    for head in range(local_heads):
        logits = masked_scores(queries[:, head, :], row_keys, allowed, scaling)
        peak = jnp.max(logits, axis=1, keepdims=True)
        lse = peak + jnp.log(jnp.sum(jnp.exp(logits - peak), axis=1, keepdims=True))
        weights = jnp.exp(logits - lse).astype(jnp.bfloat16)
        head_outs.append(dot_plain(weights, row_values))
        lses.append(lse)
    attended = jnp.concatenate(head_outs, axis=1).astype(jnp.bfloat16)
    proj = lax.psum(dot_last(attended, ow), "tp")
    aunit, ra = norm_parts(proj)
    h1 = block_input + aunit * g_ao
    unit2, r2 = norm_parts(h1)
    xn2 = (unit2 * g_fi).astype(jnp.bfloat16)
    gate = dot_plain(xn2, gw)
    up = dot_plain(xn2, uw)
    act, gelu_back = jax.vjp(gelu_tanh, gate)
    hidden = (act * up).astype(jnp.bfloat16)
    ffn = lax.psum(dot_last(hidden, dw), "tp")
    funit, rf = norm_parts(ffn)
    block_output = h1 + funit * g_fo
    back_keys, back_values = (row_keys, row_values)
    dg_fo = jnp.sum(out_cotangent * funit, axis=0)
    dffn = norm_back(out_cotangent * g_fo, funit, rf).astype(jnp.bfloat16)
    dhid = dot_plain(dffn, dw)
    d_down = dot_first(dffn, hidden)
    dup = (dhid * act).astype(jnp.bfloat16)
    dgate = gelu_back(dhid * up)[0].astype(jnp.bfloat16)
    d_gate_w = dot_first(xn2, dgate)
    d_up_w = dot_first(xn2, dup)
    dxn2 = lax.psum(dot_last(dgate, gw) + dot_last(dup, uw), "tp")
    dg_fi = jnp.sum(dxn2 * unit2, axis=0)
    dh1 = out_cotangent + norm_back(dxn2 * g_fi, unit2, r2)
    dg_ao = jnp.sum(dh1 * aunit, axis=0)
    dproj = norm_back(dh1 * g_ao, aunit, ra).astype(jnp.bfloat16)
    d_o_w = dot_first(dproj, attended)
    dattended = dot_plain(dproj, ow).astype(jnp.bfloat16)
    win_keys, win_values, win_allowed = (back_keys, back_values, allowed)
    key_terms = jnp.zeros((row_len, HD), jnp.float32)
    value_terms = jnp.zeros((row_len, HD), jnp.float32)
    dq_parts = []
    for head in range(local_heads):
        query_head = queries[:, head, :]
        out_head = attended[:, head * HD : (head + 1) * HD]
        dout_head = dattended[:, head * HD : (head + 1) * HD]
        logits = masked_scores(query_head, win_keys, win_allowed, scaling)
        weights = jnp.exp(logits - lses[head])
        weights_low = weights.astype(jnp.bfloat16)
        delta = jnp.sum(
            dout_head.astype(jnp.float32) * out_head.astype(jnp.float32), axis=1, keepdims=True
        )
        dprob = dot_last(dout_head, win_values)
        dscore = (weights * (dprob - delta) * scaling).astype(jnp.bfloat16)
        dq_parts.append(dot_plain(dscore, win_keys))
        key_terms = key_terms + dot_first(dscore, query_head)
        value_terms = value_terms + dot_first(weights_low, dout_head)
    dq = jnp.stack(dq_parts, axis=1)
    dqn = unrotate(dq, cosine[:, None, :], sine[:, None, :])
    dg_q = jnp.sum(dqn * qunit, axis=(0, 1))
    dqp = norm_back(dqn * g_q, qunit, rq).reshape(tokens, local_heads * HD).astype(jnp.bfloat16)
    dkeys, dvalues = (
        lax.psum_scatter(key_terms, ("ctx", "tp"), scatter_dimension=0, tiled=True),
        lax.psum_scatter(value_terms, ("ctx", "tp"), scatter_dimension=0, tiled=True),
    )
    kunit_rows = lax.dynamic_slice_in_dim(kunit, my_sub, piece, 0)
    rk_rows = lax.dynamic_slice_in_dim(rk, my_sub, piece, 0)
    cos_rows = lax.dynamic_slice_in_dim(cosine, my_sub, piece, 0)
    sin_rows = lax.dynamic_slice_in_dim(sine, my_sub, piece, 0)
    xn1_rows = lax.dynamic_slice_in_dim(xn1, my_sub, piece, 0)
    dkn = unrotate(dkeys, cos_rows, sin_rows)
    dg_k = jnp.sum(dkn * kunit_rows, axis=0)
    dkp = norm_back(dkn * g_k, kunit_rows, rk_rows).astype(jnp.bfloat16)
    dvr = dvalues.astype(jnp.bfloat16)
    shared_part = dot_last(dkp, kw) + dot_last(dvr, vw)
    placed = lax.dynamic_update_slice(
        jnp.zeros((tokens, width), jnp.float32), shared_part, (my_sub, jnp.zeros((), jnp.int32))
    )
    dxn1 = lax.psum(dot_last(dqp, qw) + placed, "tp")
    d_q_w = dot_first(xn1, dqp)
    d_k_w = dot_first(xn1_rows, dkp)
    d_v_w = dot_first(xn1_rows, dvr)
    dg_ai = jnp.sum(dxn1 * unit1, axis=0)
    input_grad = dh1 + norm_back(dxn1 * g_ai, unit1, r1)
    rows = (
        lax.psum_scatter(d_q_w, "shard", scatter_dimension=0, tiled=True),
        lax.psum_scatter(d_k_w, "shard", scatter_dimension=0, tiled=True),
        lax.psum_scatter(d_v_w, "shard", scatter_dimension=0, tiled=True),
        lax.psum_scatter(d_o_w, "shard", scatter_dimension=0, tiled=True),
        lax.psum_scatter(d_gate_w, "shard", scatter_dimension=0, tiled=True),
        lax.psum_scatter(d_up_w, "shard", scatter_dimension=0, tiled=True),
        lax.psum_scatter(d_down, "shard", scatter_dimension=0, tiled=True),
        lax.psum_scatter(dg_ai, "shard", scatter_dimension=0, tiled=True),
        lax.psum_scatter(dg_ao, "shard", scatter_dimension=0, tiled=True),
        lax.psum_scatter(dg_fi, "shard", scatter_dimension=0, tiled=True),
        lax.psum_scatter(dg_fo, "shard", scatter_dimension=0, tiled=True),
        lax.psum_scatter(dg_q, "shard", scatter_dimension=0, tiled=True),
        lax.psum_scatter(dg_k, "shard", scatter_dimension=0, tiled=True),
    )
    split_sums = lax.psum(
        (rows[0], rows[3], rows[4], rows[5], rows[6], rows[7], rows[8], rows[9], rows[10]), "ctx"
    )
    shared_sums = lax.psum((rows[1], rows[2], rows[11], rows[12]), ("ctx", "tp"))
    return (
        block_output,
        input_grad,
        split_sums[0],
        shared_sums[0],
        shared_sums[1],
        split_sums[1],
        split_sums[2],
        split_sums[3],
        split_sums[4],
        split_sums[5],
        split_sums[6],
        split_sums[7],
        split_sums[8],
        shared_sums[2],
        shared_sums[3],
    )


def solution(mesh):
    placed = (
        P(("shard", "ctx"), None),
        P(("shard", "ctx"), None),
        P("shard", None),
        P("shard", "tp"),
        P("shard", None),
        P("shard", None),
        P("shard", "tp"),
        P("shard", "tp"),
        P("shard", "tp"),
        P("shard", "tp"),
        P("shard"),
        P("shard"),
        P("shard"),
        P("shard"),
        P("shard"),
        P("shard"),
    )
    return jax.shard_map(
        per_device,
        mesh=mesh,
        in_specs=placed,
        out_specs=(
            P(("shard", "ctx"), None),
            P(("shard", "ctx"), None),
            P("shard", "tp"),
            P("shard", None),
            P("shard", None),
            P("shard", "tp"),
            P("shard", "tp"),
            P("shard", "tp"),
            P("shard", "tp"),
            P("shard"),
            P("shard"),
            P("shard"),
            P("shard"),
            P("shard"),
            P("shard"),
        ),
        check_vma=False,
    )
```

profile of v0, /device:TPU:0, one launch (start us, length us, event | category | flops | bytes accessed | tf_op | source)
XLA Modules:
  0.0 787.6 jit_solution(877558683739222252)
XLA Ops:
  15.8 13.9 %all-reduce.17 = (bf16[640]{0:T(1024)(128)(2,1)S(1)}, bf16[256]{0:T(256)(128)(2,1)S(1)}, bf16[256]{0:T(256)(128)(2,1)S(1)}, bf16[640]{0:T(1024)(128)(2,1)S(1)}, ...) all-reduce(bf16[640]{0:T(1024)(128)(2,1)S(1)} %dynamic-update-slice, ...), channel_id=1, replica_groups=mesh['shard'=4,'ctx'=4,'tp'=2] {'shard'}, use_global_device_ids=true, to_apply=%add | all-reduce | flops 3072 | bytes 12288
  32.4 14.4 %all_gather.48 = bf16[640,256]{1,0:T(8,128)(2,1)S(1)} all-gather(bf16[160,256]{1,0:T(8,128)(2,1)} %param.20), channel_id=1, replica_groups=mesh['shard'=4,'ctx'=4,'tp'=2] {'shard'}, dimensions={0}, use_global_device_ids=true | all-gather | bytes 409600 | tf_op jit(solution)/shard_map/all_gather | solution.py:115
  49.5 5.8 all_gather.50
  55.3 17.0 %all_gather.46 = bf16[640,512]{1,0:T(8,128)(2,1)S(1)} all-gather(bf16[160,512]{1,0:T(8,128)(2,1)S(1)} %copy-done.46), channel_id=1, replica_groups=mesh['shard'=4,'ctx'=4,'tp'=2] {'shard'}, dimensions={0}, use_global_device_ids=true | all-gather | bytes 819200 | tf_op jit(solution)/shard_map/all_gather | solution.py:114
  74.1 16.6 %all_gather.53 = bf16[640,512]{1,0:T(8,128)(2,1)S(1)} all-gather(bf16[160,512]{1,0:T(8,128)(2,1)S(1)} %copy-done.47), channel_id=1, replica_groups=mesh['shard'=4,'ctx'=4,'tp'=2] {'shard'}, dimensions={0}, use_global_device_ids=true | all-gather | bytes 819200 | tf_op jit(solution)/shard_map/all_gather | solution.py:117
  90.7 14.7 %all_gather.51 = bf16[640,256]{1,0:T(8,128)(2,1)S(1)} all-gather(bf16[160,256]{1,0:T(8,128)(2,1)S(1)} %copy-done.48), channel_id=1, replica_groups=mesh['shard'=4,'ctx'=4,'tp'=2] {'shard'}, dimensions={0}, use_global_device_ids=true | all-gather | bytes 409600 | tf_op jit(solution)/shard_map/all_gather | solution.py:116
  105.6 5.8 all_gather.52
  116.3 22.7 %all-reduce.25.cloned.1.call-done = f32[128,640]{1,0:T(8,128)} async-done(((f32[128,640]{1,0:T(8,128)}), f32[128,640]{1,0:T(8,128)}) %all-reduce.25.cloned.1.call-update) | async-done | bytes 327696 | tf_op jit(solution)/shard_map/psum | solution.py:154
  141.4 7.5 all-gather.4.cloned.1.call-done
  148.8 2.5 fusion.58
  151.3 30.5 %all-gather.6.cloned.1.call-done = bf16[640,1024]{1,0:T(8,128)(2,1)} async-done(((bf16[160,1024]{1,0:T(8,128)(2,1)}), bf16[640,1024]{1,0:T(8,128)(2,1)}) %all-gather.6.cloned.1.call-update) | async-done | bytes 1310736 | tf_op jit(solution)/shard_map/all_gather | solution.py:119
  181.8 2.7 multiply_convert_fusion.1
  184.5 30.3 %all-gather.8.cloned.1.call-done = bf16[640,1024]{1,0:T(8,128)(2,1)} async-done(((bf16[160,1024]{1,0:T(8,128)(2,1)}), bf16[640,1024]{1,0:T(8,128)(2,1)}) %all-gather.8.cloned.1.call-update) | async-done | bytes 1310736 | tf_op jit(solution)/shard_map/all_gather | solution.py:120
  214.8 2.7 fusion.59
  217.5 23.6 %all-reduce.27.cloned.1.call-done = f32[128,640]{1,0:T(8,128)} async-done(((f32[128,640]{1,0:T(8,128)}), f32[128,640]{1,0:T(8,128)}) %all-reduce.27.cloned.1.call-update) | async-done | bytes 327696 | tf_op jit(solution)/shard_map/psum | solution.py:163
  249.1 24.5 %all-reduce.29.cloned.1.call-done = f32[128,640]{1,0:T(8,128)} async-done(((f32[128,640]{1,0:T(8,128)}), f32[128,640]{1,0:T(8,128)}) %all-reduce.29.cloned.1.call-update) | async-done | bytes 327696 | tf_op jit(solution)/shard_map/psum | solution.py:175
  280.3 32.6 %reduce-scatter.10.cloned.1.call-done = f32[64,256]{1,0:T(8,128)} async-done(((f32[512,256]{1,0:T(8,128)}), f32[64,256]{1,0:T(8,128)}) %reduce-scatter.10.cloned.1.call-update) | async-done | bytes 65552 | tf_op jit(solution)/shard_map/reduce_scatter | solution.py:206
  315.7 34.8 %reduce-scatter.12.cloned.1.call-done = f32[64,256]{1,0:T(8,128)} async-done(((f32[512,256]{1,0:T(8,128)}), f32[64,256]{1,0:T(8,128)}) %reduce-scatter.12.cloned.1.call-update) | async-done | bytes 65552 | tf_op jit(solution)/shard_map/reduce_scatter | solution.py:207
  359.8 2.1 fusion.65
  367.2 8.7 %reduce-scatter.16.cloned.1.call-done = f32[160,256]{1,0:T(8,128)} async-done(((f32[640,256]{1,0:T(8,128)}), f32[160,256]{1,0:T(8,128)}) %reduce-scatter.16.cloned.1.call-update) | async-done | bytes 163856 | tf_op jit(solution)/shard_map/reduce_scatter | solution.py:230
  375.8 24.1 %reduce-scatter.18.cloned.1.call-done = f32[160,256]{1,0:T(8,128)} async-done(((f32[640,256]{1,0:T(8,128)}), f32[160,256]{1,0:T(8,128)}) %reduce-scatter.18.cloned.1.call-update) | async-done | bytes 163856 | tf_op jit(solution)/shard_map/reduce_scatter | solution.py:231
  400.1 32.3 %reduce-scatter.14.cloned.1.call-done = f32[160,512]{1,0:T(8,128)} async-done(((f32[640,512]{1,0:T(8,128)}), f32[160,512]{1,0:T(8,128)}) %reduce-scatter.14.cloned.1.call-update) | async-done | bytes 327696 | tf_op jit(solution)/shard_map/reduce_scatter | solution.py:229
  432.3 32.4 %reduce-scatter.20.cloned.1.call-done = f32[160,512]{1,0:T(8,128)} async-done(((f32[640,512]{1,0:T(8,128)}), f32[160,512]{1,0:T(8,128)}) %reduce-scatter.20.cloned.1.call-update) | async-done | bytes 327696 | tf_op jit(solution)/shard_map/reduce_scatter | solution.py:232
  464.7 53.1 %reduce-scatter.22.cloned.1.call-done = f32[160,1024]{1,0:T(8,128)} async-done(((f32[640,1024]{1,0:T(8,128)}), f32[160,1024]{1,0:T(8,128)}) %reduce-scatter.22.cloned.1.call-update) | async-done | bytes 655376 | tf_op jit(solution)/shard_map/reduce_scatter | solution.py:233
  517.8 54.1 %reduce-scatter.24.cloned.1.call-done = f32[160,1024]{1,0:T(8,128)} async-done(((f32[640,1024]{1,0:T(8,128)}), f32[160,1024]{1,0:T(8,128)}) %reduce-scatter.24.cloned.1.call-update) | async-done | bytes 655376 | tf_op jit(solution)/shard_map/reduce_scatter | solution.py:234
  572.0 54.0 %reduce-scatter.26.cloned.1.call-done = f32[160,1024]{1,0:T(8,128)} async-done(((f32[640,1024]{1,0:T(8,128)}), f32[160,1024]{1,0:T(8,128)}) %reduce-scatter.26.cloned.1.call-update) | async-done | bytes 655376 | tf_op jit(solution)/shard_map/reduce_scatter | solution.py:235
  627.4 25.4 %all-reduce.31.cloned.1.call-done = f32[128,640]{1,0:T(8,128)} async-done(((f32[128,640]{1,0:T(8,128)}), f32[128,640]{1,0:T(8,128)}) %all-reduce.31.cloned.1.call-update) | async-done | bytes 327696 | tf_op jit(solution)/shard_map/psum | solution.py:222
  654.0 19.0 %all-reduce.16 = (f32[640]{0:T(1024)S(1)}, f32[640]{0:T(1024)S(1)}, f32[640]{0:T(1024)S(1)}, f32[640]{0:T(1024)S(1)}, f32[256]{0:T(256)S(1)}, /*index=5*/f32[256]{0:T(256)S(1)}) all-reduce(f32[640]{0:T(1024)S(1)} %get-tuple-element.21, f32[640]{0:T(1024)S(1)} %get-tuple-element.19, ...), channel_id=11, replica_groups=mesh['shard'=4,'ctx'=4,'tp'=2] {'shard'}, use_global_device_ids=true, to_apply=%region_42.43.clone | all-reduce | flops 3072 | bytes 24576
  673.4 13.0 %all-reduce.12 = (f32[64]{0:T(128)}, f32[64]{0:T(128)}) all-reduce(f32[64]{0:T(128)S(1)} %dynamic-slice.20, f32[64]{0:T(128)S(1)} %dynamic-slice.22), channel_id=1, replica_groups=mesh['shard'=4,'ctx'=4,'tp'=2] {'ctx','tp'}, use_global_device_ids=true, to_apply=%region_56.57 | all-reduce | flops 128 | bytes 1024 | tf_op jit(solution)/shard_map/psum | solution.py:246
  686.3 7.6 all-reduce.14
  695.8 14.3 %all-reduce.33.cloned.1.call-done = (f32[160,256]{1,0:T(8,128)}, f32[160,256]{1,0:T(8,128)}) async-done(((f32[160,256]{1,0:T(8,128)}, f32[160,256]{1,0:T(8,128)}), (f32[160,256]{1,0:T(8,128)}, f32[160,256]{1,0:T(8,128)})) %all-reduce.33.cloned.1.call-update) | async-done | bytes 327696 | tf_op jit(solution)/shard_map/psum | solution.py:246
  710.1 61.9 %all-reduce.35.cloned.1.call-done = (f32[160,512]{1,0:T(8,128)}, f32[160,512]{1,0:T(8,128)}, f32[160,1024]{1,0:T(8,128)}, f32[160,1024]{1,0:T(8,128)}, f32[160,1024]{1,0:T(8,128)}) async-done(((f32[160,512]{1,0:T(8,128)}, f32[160,512]{1,0:T(8,128)}, f32[160,1024]{1,0:T(8,128)}, f32[160,1024]{1,0:T(8,128)}, f32[160,1024]{1,0:T(8,128)}), (f32[160,512]{1,0:T(8,128)}, f32[160,512]{1,0:T(8,128)}, ...) | async-done | bytes 2621456 | tf_op jit(solution)/shard_map/psum | solution.py:243
  (270 shorter events, 64.1 us)
Async XLA Ops:
  8.0 130.9 %all-reduce.25.cloned.1.call-start = ((), (), s32[]{:S(2)}) async-start(), calls=%async_computation.9 | async-start | bytes 655360 | tf_op jit(solution)/shard_map/psum | solution.py:154
  30.8 24.5 %copy-start.49 = (f32[128]{0:T(128)}, f32[128]{0:T(128)S(1)}, u32[]{:S(2)}) copy-start(f32[128]{0:T(128)S(1)} %add_rsqrt_fusion.5) | copy-start | bytes 1540
  46.8 25.5 %copy-start.11 = (bf16[640,256]{1,0:T(8,128)(2,1)}, bf16[640,256]{1,0:T(8,128)(2,1)S(1)}, u32[]{:S(2)}) copy-start(bf16[640,256]{1,0:T(8,128)(2,1)S(1)} %all_gather.48) | copy-start | bytes 983044
  48.3 24.3 %copy-start.53 = (f32[128]{0:T(128)}, f32[128]{0:T(128)S(1)}, u32[]{:S(2)}) copy-start(f32[128]{0:T(128)S(1)} %add_rsqrt_fusion.4) | copy-start | bytes 1540
  49.5 23.8 %copy-start.29 = (f32[128,128]{1,0:T(8,128)}, f32[128,128]{1,0:T(8,128)S(1)}, u32[]{:S(2)}) copy-start(f32[128,128]{1,0:T(8,128)S(1)} %get-tuple-element.75) | copy-start | bytes 196612
  73.4 32.0 %copy-start.40 = (bf16[128,2,128]{2,0,1:T(8,128)(2,1)}, bf16[128,2,128]{2,0,1:T(8,128)(2,1)S(1)}, u32[]{:S(2)}) copy-start(bf16[128,2,128]{2,0,1:T(8,128)(2,1)S(1)} %get-tuple-element.66) | copy-start | bytes 196612
  113.3 26.7 %copy-start = (f32[128,640]{1,0:T(8,128)S(1)}, f32[128,640]{1,0:T(8,128)}, u32[]{:S(2)}) copy-start(f32[128,640]{1,0:T(8,128)} %param.16) | copy-start | bytes 983044
  114.4 34.4 %all-gather.4.cloned.1.call-start = ((), (), s32[]{:S(2)}) async-start(), calls=%async_computation.10 | async-start | bytes 1638400 | tf_op jit(solution)/shard_map/all_gather | solution.py:118
  115.0 66.8 %all-gather.6.cloned.1.call-start = ((), (), s32[]{:S(2)}) async-start(), calls=%async_computation.11 | async-start | bytes 1638400 | tf_op jit(solution)/shard_map/all_gather | solution.py:119
  115.6 99.1 %all-gather.8.cloned.1.call-start = ((), (), s32[]{:S(2)}) async-start(), calls=%async_computation.12 | async-start | bytes 1638400 | tf_op jit(solution)/shard_map/all_gather | solution.py:120
  116.2 125.0 %all-reduce.27.cloned.1.call-start = ((), (), s32[]{:S(2)}) async-start(), calls=%async_computation.13 | async-start | bytes 655360 | tf_op jit(solution)/shard_map/psum | solution.py:163
  141.3 43.2 %copy-start.4 = (bf16[128,640]{1,0:T(8,128)(2,1)}, bf16[128,640]{1,0:T(8,128)(2,1)S(1)}, u32[]{:S(2)}) copy-start(bf16[128,640]{1,0:T(8,128)(2,1)S(1)} %multiply_convert_fusion.4) | copy-start | bytes 491524
  214.8 27.7 %copy-start.6 = (f32[128,640]{1,0:T(8,128)S(1)}, f32[128,640]{1,0:T(8,128)}, u32[]{:S(2)}) copy-start(f32[128,640]{1,0:T(8,128)} %param.17) | copy-start | bytes 983044
  217.5 56.1 %all-reduce.29.cloned.1.call-start = ((), (), s32[]{:S(2)}) async-start(), calls=%async_computation.14 | async-start | bytes 655360 | tf_op jit(solution)/shard_map/psum | solution.py:175
  247.7 27.0 %copy-start.1 = (f32[128,640]{1,0:T(8,128)S(1)}, f32[128,640]{1,0:T(8,128)}, u32[]{:S(2)}) copy-start(f32[128,640]{1,0:T(8,128)} %all-reduce.25.cloned.1.call-done) | copy-start | bytes 983044
  249.1 63.8 %reduce-scatter.10.cloned.1.call-start = ((), (), s32[]{:S(2)}) async-start(), calls=%async_computation.15 | async-start | bytes 589824 | tf_op jit(solution)/shard_map/reduce_scatter | solution.py:206
  278.6 71.9 %reduce-scatter.12.cloned.1.call-start = ((), (), s32[]{:S(2)}) async-start(), calls=%async_computation.16 | async-start | bytes 589824 | tf_op jit(solution)/shard_map/reduce_scatter | solution.py:207
  278.8 34.1 %copy-start.30 = (f32[128,128]{1,0:T(8,128)S(1)}, f32[128,128]{1,0:T(8,128)}, u32[]{:S(2)}) copy-start(f32[128,128]{1,0:T(8,128)} %copy-done.29) | copy-start | bytes 196612
  278.8 34.1 %copy-start.32 = (f32[128,128]{1,0:T(8,128)S(1)}, f32[128,128]{1,0:T(8,128)}, u32[]{:S(2)}) copy-start(f32[128,128]{1,0:T(8,128)} %copy-done.31) | copy-start | bytes 196612
  278.8 34.9 %copy-start.42 = (f32[128,256]{1,0:T(8,128)S(1)}, f32[128,256]{1,0:T(8,128)}, u32[]{:S(2)}) copy-start(f32[128,256]{1,0:T(8,128)} %get-tuple-element.58) | copy-start | bytes 393220
  280.3 95.6 %reduce-scatter.16.cloned.1.call-start = ((), (), s32[]{:S(2)}) async-start(), calls=%async_computation.19 | async-start | bytes 819200 | tf_op jit(solution)/shard_map/reduce_scatter | solution.py:230
  315.1 84.9 %reduce-scatter.18.cloned.1.call-start = ((), (), s32[]{:S(2)}) async-start(), calls=%async_computation.20 | async-start | bytes 819200 | tf_op jit(solution)/shard_map/reduce_scatter | solution.py:231
  352.5 79.8 %reduce-scatter.14.cloned.1.call-start = ((), (), s32[]{:S(2)}) async-start(), calls=%async_computation.18 | async-start | bytes 1638400 | tf_op jit(solution)/shard_map/reduce_scatter | solution.py:229
  355.1 109.6 %reduce-scatter.20.cloned.1.call-start = ((), (), s32[]{:S(2)}) async-start(), calls=%async_computation.21 | async-start | bytes 1638400 | tf_op jit(solution)/shard_map/reduce_scatter | solution.py:232
  356.8 161.0 %reduce-scatter.22.cloned.1.call-start = ((), (), s32[]{:S(2)}) async-start(), calls=%async_computation.22 | async-start | bytes 3276800 | tf_op jit(solution)/shard_map/reduce_scatter | solution.py:233
  358.9 213.1 %reduce-scatter.24.cloned.1.call-start = ((), (), s32[]{:S(2)}) async-start(), calls=%async_computation.23 | async-start | bytes 3276800 | tf_op jit(solution)/shard_map/reduce_scatter | solution.py:234
  361.9 264.0 %reduce-scatter.26.cloned.1.call-start = ((), (), s32[]{:S(2)}) async-start(), calls=%async_computation.24 | async-start | bytes 3276800 | tf_op jit(solution)/shard_map/reduce_scatter | solution.py:235
  365.0 287.8 %all-reduce.31.cloned.1.call-start = ((), (), s32[]{:S(2)}) async-start(), calls=%async_computation.17 | async-start | bytes 655360 | tf_op jit(solution)/shard_map/psum | solution.py:222
  367.1 343.0 %all-reduce.33.cloned.1.call-start = ((), (), s32[]{:S(2)}) async-start(), calls=%async_computation.25 | async-start | bytes 655360 | tf_op jit(solution)/shard_map/psum | solution.py:246
  400.0 372.0 %all-reduce.35.cloned.1.call-start = ((), (), s32[]{:S(2)}) async-start(), calls=%async_computation.26 | async-start | bytes 5242880 | tf_op jit(solution)/shard_map/psum | solution.py:243
  626.0 26.8 %copy-start.50 = (f32[128]{0:T(128)S(1)}, f32[128]{0:T(128)}, u32[]{:S(2)}) copy-start(f32[128]{0:T(128)} %copy-done.49) | copy-start | bytes 1540
  626.0 68.0 %copy-start.8 = (f32[128,640]{1,0:T(8,128)S(1)}, f32[128,640]{1,0:T(8,128)}, u32[]{:S(2)}) copy-start(f32[128,640]{1,0:T(8,128)} %copy-done.7) | copy-start | bytes 983044
  (41 other events, 155.6 us)
Sparse Core Ops, SparseCore 0:
  114.5 24.3 all-reduce.24
  217.6 23.4 all-reduce.26
  249.2 24.3 all-reduce.28
  278.7 34.1 reduce-scatter.9
  316.4 34.0 reduce-scatter.11
  353.3 22.5 reduce-scatter.15
  378.7 21.2 reduce-scatter.17
  402.3 30.0 reduce-scatter.13
  434.6 30.0 reduce-scatter.19
  466.9 50.9 reduce-scatter.21
  520.1 51.7 reduce-scatter.23
  574.1 51.7 reduce-scatter.25
  628.8 23.8 all-reduce.30
  655.7 54.3 all-reduce.32
  712.6 59.3 all-reduce.34
Sparse Core Ops, SparseCore 1:
  116.5 32.3 all-gather.3
  150.3 31.5 all-gather.5
  183.2 31.5 all-gather.7
where the time goes:
time: 789 us; the launch traced here: 788 us
  waiting for transfers between devices  568 us (72%)
  blocking collectives  128 us (16%)
  matrix products  30.1 us (4%)
  local copies, waits for them, and re-layouts  21.5 us (3%)
  other arithmetic  19.7 us (2%)
  between operations  19.2 us (2%)
    psum x1, waiting for transfers between devices, per_device(): lax.psum((rows[0], rows[3], rows[4], rows[5], rows[6], rows[7], rows[8],...  61.9 us
    reduce_scatter x1, waiting for transfers between devices, per_device(): lax.psum_scatter(d_up_w, 'shard', scatter_dimension=0, tiled=True)  54.1 us
    reduce_scatter x1, waiting for transfers between devices, per_device(): lax.psum_scatter(d_down, 'shard', scatter_dimension=0, tiled=True)  54 us
    reduce_scatter x1, waiting for transfers between devices, per_device(): lax.psum_scatter(d_gate_w, 'shard', scatter_dimension=0, tiled=True)  53.1 us
    reduce_scatter x1, waiting for transfers between devices, per_device(): lax.psum_scatter(value_terms, ('ctx', 'tp'), scatter_dimension=0, tiled=T...  34.8 us
    unnamed x2, blocking collectives  32.9 us
    reduce_scatter x1, waiting for transfers between devices, per_device(): lax.psum_scatter(key_terms, ('ctx', 'tp'), scatter_dimension=0, tiled=True)  32.6 us
    reduce_scatter x1, waiting for transfers between devices, per_device(): lax.psum_scatter(d_o_w, 'shard', scatter_dimension=0, tiled=True)  32.4 us
  transfers between devices with their start and end apart: 18, of which 18 were waited for; matrix products, arithmetic and copies ran while one was open for 4% of the time, Pallas kernels for 0%

commit v1 on v0

v1 whole, which is shorter than its diff:
```python
import functools

import jax
import jax.numpy as jnp
from jax import lax
from jax.experimental import pallas as pl
from jax.experimental.pallas import tpu as pltpu
from jax.sharding import PartitionSpec as P

HD = 256


eps = 1e-06
rope_base = 1000000.0


def dot_plain(left, right):
    return jnp.dot(left, right, preferred_element_type=jnp.float32)


def dot_last(left, right):
    return lax.dot_general(
        left, right, (((1,), (1,)), ((), ())), preferred_element_type=jnp.float32
    )


def dot_first(left, right):
    return lax.dot_general(
        left, right, (((0,), (0,)), ((), ())), preferred_element_type=jnp.float32
    )


def norm_parts(value):
    scale = lax.rsqrt(jnp.mean(value * value, axis=-1, keepdims=True) + eps)
    return (value * scale, scale)


def norm_back(dnormed, unit, scale):
    return scale * (dnormed - unit * jnp.mean(dnormed * unit, axis=-1, keepdims=True))


def rope_tables(position):
    freq = rope_base ** (-jnp.arange(HD // 2).astype(jnp.float32) * (2.0 / HD))
    angle = position.astype(jnp.float32)[:, None] * freq[None, :]
    return (jnp.cos(angle), jnp.sin(angle))


def rotate(value, cosine, sine):
    half = value.shape[-1] // 2
    first, second = (value[..., :half], value[..., half:])
    return jnp.concatenate(
        [first * cosine - second * sine, second * cosine + first * sine], axis=-1
    )


def unrotate(value, cosine, sine):
    half = value.shape[-1] // 2
    first, second = (value[..., :half], value[..., half:])
    return jnp.concatenate(
        [first * cosine + second * sine, second * cosine - first * sine], axis=-1
    )


def layout(lengths, count):
    index = jnp.arange(count)
    ends = jnp.cumsum(lengths)
    after = (index[:, None] >= ends[None, :]).astype(jnp.int32)
    segment = jnp.sum(after, axis=1)
    position = index - jnp.sum(after * lengths[None, :], axis=1)
    return (segment, position)


def gelu_tanh(value):
    return jax.nn.gelu(value, approximate=True)


def masked_scores(query_head, key_block, mask, scaling):
    raw = dot_last(query_head, key_block) * scaling
    return jnp.where(mask, raw, -1e30)

MESH = pl.DeviceIdType.MESH
LANES = 128
WAYS = 4


def vmem():
    return pl.BlockSpec(memory_space=pltpu.VMEM)


def greet(peers):
    barrier = pltpu.get_barrier_semaphore()
    for peer in peers:
        pl.semaphore_signal(barrier, inc=1, device_id=peer, device_id_type=MESH)
    pl.semaphore_wait(barrier, len(peers))


def params(number):
    return pltpu.CompilerParams(
        collective_id=number, has_side_effects=True, vmem_limit_bytes=56 * 1024 * 1024
    )


def send(src, dst, sems, where, peer):
    copy = pltpu.make_async_remote_copy(
        src_ref=src,
        dst_ref=dst,
        send_sem=sems[0].at[where],
        recv_sem=sems[1].at[where],
        device_id=peer,
        device_id_type=MESH,
    )
    copy.start()
    return copy


def place(n_ctx):
    shard, ctx, tp = (lax.axis_index("shard"), lax.axis_index("ctx"), lax.axis_index("tp"))
    core = lax.rem(ctx, 2)
    high = lax.rem(lax.div(ctx, 2), 2)
    return shard, ctx, tp, ctx + 1 - 2 * core, ctx + 2 - 4 * high


def columns(member, width):
    return pl.ds(pl.multiple_of(member * width, LANES), width)


def block_rows(index, count):
    return pl.ds(pl.multiple_of(index * count, 8), count)


def gather_kernel(n_shard, n_ctx, count, *refs):
    weights, unit, gain = (refs[:count], refs[count], refs[count + 1])
    refs = refs[count + 2 :]
    outs, row, gains = (refs[:count], refs[count], refs[count + 1])
    sems_a, sems_n, sems_f, sems_c, sems_x, sems_g, local = (
        refs[count + 2 : count + 4],
        refs[count + 4 : count + 6],
        refs[count + 6 : count + 8],
        refs[count + 8 : count + 10],
        refs[count + 10 : count + 12],
        refs[count + 12 : count + 14],
        refs[count + 14],
    )
    shard, ctx, tp, near, far = place(n_ctx)
    member = lax.rem(ctx, WAYS)
    rows = weights[0].shape[0]
    tokens = unit.shape[0]
    widths = [item.shape[1] // WAYS for item in weights]
    peers = [(lax.rem(shard + d, n_shard), ctx, tp) for d in range(1, n_shard)]
    mates = [(shard, lax.rem(ctx + d, n_ctx), tp) for d in range(1, n_ctx)]
    greet(peers + mates)
    started = []
    first = {}
    for d in range(1, n_shard):
        for a in range(count):
            cols = columns(member, widths[a])
            first[d, a] = send(
                weights[a].at[:, cols],
                outs[a].at[block_rows(shard, rows), cols],
                sems_a,
                (d - 1, a),
                peers[d - 1],
            )
        started.append(send(gain, gains.at[shard], sems_g, d - 1, peers[d - 1]))
    for d in range(1, n_ctx):
        started.append(
            send(unit, row.at[block_rows(ctx, tokens)], sems_x, d - 1, mates[d - 1])
        )
    own = [
        pltpu.make_async_copy(weights[a], outs[a].at[block_rows(shard, rows)], local.at[a])
        for a in range(count)
    ]
    own.append(pltpu.make_async_copy(unit, row.at[block_rows(ctx, tokens)], local.at[count]))
    own.append(pltpu.make_async_copy(gain, gains.at[shard], local.at[count + 1]))
    for item in own:
        item.start()
    across = {}
    for d in range(1, n_shard):
        source = lax.rem(shard - d + n_shard, n_shard)
        for a in range(count):
            first[d, a].wait_recv()
            block = outs[a].at[block_rows(source, rows), columns(member, widths[a])]
            across[d, a] = send(block, block, sems_f, (d - 1, a), (shard, far, tp))
            started.append(send(block, block, sems_n, (d - 1, a), (shard, near, tp)))
    other = lax.rem(far, WAYS)
    for d in range(1, n_shard):
        source = lax.rem(shard - d + n_shard, n_shard)
        for a in range(count):
            across[d, a].wait_recv()
            block = outs[a].at[block_rows(source, rows), columns(other, widths[a])]
            started.append(send(block, block, sems_c, (d - 1, a), (shard, near, tp)))
    for item in started:
        item.wait()
    for item in list(first.values()) + list(across.values()):
        item.wait_send()
    for item in own:
        item.wait()


def gather_all(n_shard, n_ctx, weights, unit, gain):
    count = len(weights)
    grid = pltpu.SemaphoreType.DMA((n_shard - 1, count))
    return pl.pallas_call(
        functools.partial(gather_kernel, n_shard, n_ctx, count),
        out_shape=[
            jax.ShapeDtypeStruct((item.shape[0] * n_shard, item.shape[1]), item.dtype)
            for item in weights
        ]
        + [
            jax.ShapeDtypeStruct((unit.shape[0] * n_ctx, unit.shape[1]), unit.dtype),
            jax.ShapeDtypeStruct((n_shard,) + gain.shape, gain.dtype),
        ],
        in_specs=[vmem()] * (count + 2),
        out_specs=[vmem()] * (count + 2),
        scratch_shapes=[grid] * 8
        + [pltpu.SemaphoreType.DMA((n_ctx - 1,))] * 2
        + [pltpu.SemaphoreType.DMA((n_shard - 1,))] * 2
        + [pltpu.SemaphoreType.DMA((count + 2,))],
        compiler_params=params(0),
        name="gather_all",
    )(*weights, unit, gain)


def tp_kernel(n_tp, part, out, inbox, send_sem, recv_sem):
    shard, ctx, tp = (lax.axis_index("shard"), lax.axis_index("ctx"), lax.axis_index("tp"))
    peers = [(shard, ctx, lax.rem(tp + d, n_tp)) for d in range(1, n_tp)]
    greet(peers)
    copies = [
        send(part, inbox.at[d - 1], (send_sem, recv_sem), d - 1, peers[d - 1])
        for d in range(1, n_tp)
    ]
    total = part[...].astype(jnp.float32)
    for d in range(1, n_tp):
        copies[d - 1].wait_recv()
        total = total + inbox[d - 1].astype(jnp.float32)
    out[...] = total
    for copy in copies:
        copy.wait_send()


def tp_sum(value, n_tp, number):
    part = value.astype(jnp.bfloat16)
    return pl.pallas_call(
        functools.partial(tp_kernel, n_tp),
        out_shape=jax.ShapeDtypeStruct(part.shape, jnp.float32),
        in_specs=[vmem()],
        out_specs=vmem(),
        scratch_shapes=[
            pltpu.VMEM((n_tp - 1,) + part.shape, jnp.bfloat16),
            pltpu.SemaphoreType.DMA((n_tp - 1,)),
            pltpu.SemaphoreType.DMA((n_tp - 1,)),
        ],
        compiler_params=params(number),
        name=f"tp_sum{number}",
    )(part)


def ctx_kernel(n_ctx, part, out, inbox, send_sem, recv_sem):
    shard, ctx, tp = (lax.axis_index("shard"), lax.axis_index("ctx"), lax.axis_index("tp"))
    tokens = out.shape[0]
    peers = [(shard, lax.rem(ctx + d, n_ctx), tp) for d in range(1, n_ctx)]
    greet(peers)
    copies = [
        send(
            part.at[block_rows(peers[d - 1][1], tokens)],
            inbox.at[d - 1],
            (send_sem, recv_sem),
            d - 1,
            peers[d - 1],
        )
        for d in range(1, n_ctx)
    ]
    total = part[block_rows(ctx, tokens), :].astype(jnp.float32)
    for d in range(1, n_ctx):
        copies[d - 1].wait_recv()
        total = total + inbox[d - 1].astype(jnp.float32)
    out[...] = total
    for copy in copies:
        copy.wait_send()


def ctx_scatter(value, n_ctx, number):
    part = value.astype(jnp.bfloat16)
    piece = (part.shape[0] // n_ctx, part.shape[1])
    return pl.pallas_call(
        functools.partial(ctx_kernel, n_ctx),
        out_shape=jax.ShapeDtypeStruct(piece, jnp.float32),
        in_specs=[vmem()],
        out_specs=vmem(),
        scratch_shapes=[
            pltpu.VMEM((n_ctx - 1,) + piece, jnp.bfloat16),
            pltpu.SemaphoreType.DMA((n_ctx - 1,)),
            pltpu.SemaphoreType.DMA((n_ctx - 1,)),
        ],
        compiler_params=params(number),
        name=f"ctx_scatter{number}",
    )(part)


def grad_kernel(n_shard, n_ctx, n_tp, count, kv_at, *refs):
    grads, gain = (refs[:count], refs[count])
    refs = refs[count + 1 :]
    outs, gain_out = (refs[: count + 1], refs[count + 1])
    (half, away, inbox, mine, arrived, done, kv_in, groups_in, shared) = refs[
        count + 2 : count + 11
    ]
    (g_near, g_far, g_mid, g_shard, g_group, g_tp) = refs[count + 11 : count + 17]
    sems = refs[count + 17 :]
    pair = [(sems[2 * k], sems[2 * k + 1]) for k in range(len(sems) // 2)]
    s_core, s_far, s_shard, s_group, s_kv, s_share, s_gain, s_gz, s_gg, s_gt = pair
    shard, ctx, tp, near, far = place(n_ctx)
    n_groups = n_ctx // WAYS
    group = lax.div(ctx, WAYS)
    member, other = (lax.rem(ctx, WAYS), lax.rem(far, WAYS))
    beside = lax.rem(near, WAYS)
    opposite = beside + other - member
    rows = outs[0].shape[0]
    widths = [item.shape[1] // WAYS for item in grads]
    starts = [sum(widths[:a]) for a in range(count)]
    near_id, far_id = ((shard, near, tp), (shard, far, tp))
    z_ids = [(lax.rem(shard + d, n_shard), ctx, tp) for d in range(1, n_shard)]
    g_ids = [(shard, lax.rem(ctx + WAYS * d, n_ctx), tp) for d in range(1, n_groups)]
    t_ids = [(shard, ctx, lax.rem(tp + d, n_tp)) for d in range(1, n_tp)]
    greet([near_id, far_id] + z_ids + g_ids + t_ids)

    ends = []
    core = {}
    for slot, quarter in ((1, opposite), (0, beside)):
        for a in range(count):
            core[slot, a] = send(
                grads[a].at[:, columns(quarter, widths[a])],
                half.at[slot, :, pl.ds(starts[a], widths[a])],
                s_core,
                (slot, a),
                near_id,
            )
    gain_near = send(gain, g_near, s_gain, 0, near_id)
    order = list(range(1, n_shard)) + [0]
    targets = [lax.rem(shard + d, n_shard) for d in range(n_shard)]

    for a in range(count):
        core[1, a].wait_recv()
    over = {}
    for d in order:
        where = block_rows(targets[d], rows)
        for a in range(count):
            cols = pl.ds(starts[a], widths[a])
            total = half[1, where, cols].astype(jnp.float32) + grads[a][
                where, columns(other, widths[a])
            ].astype(jnp.float32)
            away[where, cols] = total.astype(jnp.bfloat16)
        over[d] = send(away.at[where], inbox.at[where], s_far, d, far_id)

    gain_near.wait_recv()
    g_mid[0] = gain[...] + g_near[...]
    gain_far = send(g_mid.at[0], g_far, s_gain, 1, far_id)

    for a in range(count):
        core[0, a].wait_recv()
    along = {}
    for d in order:
        where = block_rows(targets[d], rows)
        over[d].wait_recv()
        for a in range(count):
            cols = pl.ds(starts[a], widths[a])
            total = (
                half[0, where, cols].astype(jnp.float32)
                + grads[a][where, columns(member, widths[a])].astype(jnp.float32)
                + inbox[where, cols].astype(jnp.float32)
            )
            mine[where, cols] = total.astype(jnp.bfloat16)
        if d:
            along[d] = send(mine.at[where], arrived.at[d - 1], s_shard, d - 1, z_ids[d - 1])

    gain_far.wait_recv()
    g_shard[shard] = g_mid[0] + g_far[...]
    gz = [
        send(g_shard.at[shard], g_shard.at[shard], s_gz, d - 1, z_ids[d - 1])
        for d in range(1, n_shard)
    ]
    total = mine[block_rows(shard, rows), :].astype(jnp.float32)
    for d in range(1, n_shard):
        along[d].wait_recv()
        total = total + arrived[d - 1].astype(jnp.float32)
    if n_groups > 1:
        groups_in[group] = total.astype(jnp.bfloat16)
        moved = [
            send(groups_in.at[group], groups_in.at[group], s_group, d - 1, g_ids[d - 1])
            for d in range(1, n_groups)
        ]
        for item in moved:
            item.wait_recv()
        ends = ends + moved
        total = groups_in[0].astype(jnp.float32)
        for g in range(1, n_groups):
            total = total + groups_in[g].astype(jnp.float32)
    done[...] = total.astype(jnp.bfloat16)
    kv_cols = pl.ds(starts[kv_at], widths[kv_at])
    kvs = [
        send(done.at[:, kv_cols], kv_in.at[d - 1], s_kv, d - 1, t_ids[d - 1])
        for d in range(1, n_tp)
    ]
    for item in gz:
        item.wait_recv()
    total = g_shard[0]
    for k in range(1, n_shard):
        total = total + g_shard[k]
    g_group[group] = total
    gg = [
        send(g_group.at[group], g_group.at[group], s_gg, d - 1, g_ids[d - 1])
        for d in range(1, n_groups)
    ]
    for item in gg:
        item.wait_recv()
    total = g_group[0]
    for k in range(1, n_groups):
        total = total + g_group[k]
    g_tp[tp] = total
    gt = [
        send(g_tp.at[tp], g_tp.at[tp], s_gt, d - 1, t_ids[d - 1]) for d in range(1, n_tp)
    ]

    shared[member] = done[...]
    total = done[:, kv_cols].astype(jnp.float32)
    for d in range(1, n_tp):
        kvs[d - 1].wait_recv()
        total = total + kv_in[d - 1].astype(jnp.float32)
    shared[member, :, kv_cols] = total.astype(jnp.bfloat16)
    piece = shared.at[member]
    to_far = send(piece, piece, s_share, 0, far_id)
    to_near = send(piece, piece, s_share, 1, near_id)
    to_far.wait_recv()
    piece = shared.at[other]
    relay = send(piece, piece, s_share, 2, near_id)
    for item in gt:
        item.wait_recv()
    total = g_tp[0]
    for k in range(1, n_tp):
        total = total + g_tp[k]
    gain_out[...] = total
    to_near.wait_recv()
    relay.wait_recv()
    for q in range(WAYS):
        for a in range(count):
            value = shared[q, :, pl.ds(starts[a], widths[a])].astype(jnp.float32)
            if a == kv_at:
                out = outs[a] if q < WAYS // 2 else outs[count]
                out[:, pl.ds((q % (WAYS // 2)) * widths[a], widths[a])] = value
            else:
                outs[a][:, pl.ds(q * widths[a], widths[a])] = value
    ends = ends + list(core.values()) + [gain_near, gain_far, to_far, to_near, relay]
    ends = ends + list(over.values()) + list(along.values()) + kvs + gz + gg + gt
    for item in ends:
        item.wait_send()


def reduce_grads(n_shard, n_ctx, n_tp, grads, kv_at, gain):
    count = len(grads)
    deep = grads[0].shape[0]
    rows = deep // n_shard
    n_groups = n_ctx // WAYS
    wide = sum([item.shape[1] // WAYS for item in grads])
    out_widths = [item.shape[1] for item in grads]
    out_widths[kv_at] = out_widths[kv_at] // 2
    out_widths.append(out_widths[kv_at])
    low, full = (jnp.bfloat16, jnp.float32)

    def dma(*shape):
        return [pltpu.SemaphoreType.DMA(shape)] * 2

    return pl.pallas_call(
        functools.partial(grad_kernel, n_shard, n_ctx, n_tp, count, kv_at),
        out_shape=[jax.ShapeDtypeStruct((rows, item), full) for item in out_widths]
        + [jax.ShapeDtypeStruct(gain.shape, full)],
        in_specs=[vmem()] * (count + 1),
        out_specs=[vmem()] * (count + 2),
        scratch_shapes=[
            pltpu.VMEM((2, deep, wide), low),
            pltpu.VMEM((deep, wide), low),
            pltpu.VMEM((deep, wide), low),
            pltpu.VMEM((deep, wide), low),
            pltpu.VMEM((n_shard - 1, rows, wide), low),
            pltpu.VMEM((rows, wide), low),
            pltpu.VMEM((n_tp - 1, rows, grads[kv_at].shape[1] // WAYS), low),
            pltpu.VMEM((n_groups, rows, wide), low),
            pltpu.VMEM((WAYS, rows, wide), low),
            pltpu.VMEM(gain.shape, full),
            pltpu.VMEM(gain.shape, full),
            pltpu.VMEM((1,) + gain.shape, full),
            pltpu.VMEM((n_shard,) + gain.shape, full),
            pltpu.VMEM((n_groups,) + gain.shape, full),
            pltpu.VMEM((n_tp,) + gain.shape, full),
        ]
        + dma(2, count)
        + dma(n_shard)
        + dma(n_shard - 1)
        + dma(max(n_groups - 1, 1))
        + dma(n_tp - 1)
        + dma(3)
        + dma(2)
        + dma(n_shard - 1)
        + dma(max(n_groups - 1, 1))
        + dma(n_tp - 1),
        compiler_params=params(6),
        name="reduce_grads",
    )(*grads, gain)


def pack_lanes(items):
    flat = jnp.concatenate([item.astype(jnp.float32) for item in items])
    unit = 8 * LANES
    short = -flat.shape[0] % unit
    return jnp.pad(flat, (0, short)).reshape(-1, LANES)


def per_device(
    block_input,
    out_cotangent,
    seq_lengths,
    q_weight,
    k_weight,
    v_weight,
    o_weight,
    gate_weight,
    up_weight,
    down_weight,
    attn_in_gain,
    attn_out_gain,
    ffn_in_gain,
    ffn_out_gain,
    query_gain,
    key_gain,
):
    tokens = block_input.shape[0]
    width = block_input.shape[1]
    n_ctx = lax.axis_size("ctx")
    n_tp = lax.axis_size("tp")
    row_len = tokens * n_ctx
    n_shard = lax.axis_size("shard")
    my_start = lax.axis_index("ctx") * tokens
    scaling = HD ** (-0.5)
    segment, position = layout(seq_lengths[0], row_len)
    key_index = jnp.arange(row_len)
    query_index = my_start + jnp.arange(tokens)
    query_seg = lax.dynamic_slice_in_dim(segment, my_start, tokens)
    allowed = (query_seg[:, None] == segment[None, :]) & (
        key_index[None, :] <= query_index[:, None]
    )
    row_cosine, row_sine = rope_tables(position)
    cosine = lax.dynamic_slice_in_dim(row_cosine, my_start, tokens)
    sine = lax.dynamic_slice_in_dim(row_sine, my_start, tokens)
    unit1, r1 = norm_parts(block_input)
    gains = (attn_in_gain, attn_out_gain, ffn_in_gain, ffn_out_gain, query_gain, key_gain)
    qw, kvw, ow, gw, uw, dw, unit_row, packed = gather_all(
        n_shard,
        n_ctx,
        (
            q_weight,
            jnp.concatenate([k_weight, v_weight], axis=1),
            o_weight,
            gate_weight,
            up_weight,
            down_weight,
        ),
        unit1.astype(jnp.bfloat16),
        pack_lanes(gains),
    )
    packed = packed.reshape(n_shard, -1)
    split = []
    at = 0
    for item in gains:
        split.append(packed[:, at : at + item.shape[0]].reshape(-1))
        at = at + item.shape[0]
    g_ai, g_ao, g_fi, g_fo, g_q, g_k = split
    local_heads = qw.shape[1] // HD
    xn1 = (unit1 * g_ai).astype(jnp.bfloat16)
    qp = dot_plain(xn1, qw).reshape(tokens, local_heads, HD)
    qunit, rq = norm_parts(qp)
    queries = rotate(qunit * g_q, cosine[:, None, :], sine[:, None, :]).astype(jnp.bfloat16)
    xn1_row = (unit_row.astype(jnp.float32) * g_ai).astype(jnp.bfloat16)
    kvp = dot_plain(xn1_row, kvw)
    row_kunit, row_rk = norm_parts(kvp[:, :HD])
    row_keys = rotate(row_kunit * g_k, row_cosine, row_sine).astype(jnp.bfloat16)
    row_values = kvp[:, HD:].astype(jnp.bfloat16)
    kunit = lax.dynamic_slice_in_dim(row_kunit, my_start, tokens)
    rk = lax.dynamic_slice_in_dim(row_rk, my_start, tokens)
    head_outs = []
    lses = []
    for head in range(local_heads):
        logits = masked_scores(queries[:, head, :], row_keys, allowed, scaling)
        peak = jnp.max(logits, axis=1, keepdims=True)
        lse = peak + jnp.log(jnp.sum(jnp.exp(logits - peak), axis=1, keepdims=True))
        weights = jnp.exp(logits - lse).astype(jnp.bfloat16)
        head_outs.append(dot_plain(weights, row_values))
        lses.append(lse)
    attended = jnp.concatenate(head_outs, axis=1).astype(jnp.bfloat16)
    proj = tp_sum(dot_last(attended, ow), n_tp, 1)
    aunit, ra = norm_parts(proj)
    h1 = block_input + aunit * g_ao
    unit2, r2 = norm_parts(h1)
    xn2 = (unit2 * g_fi).astype(jnp.bfloat16)
    gate = dot_plain(xn2, gw)
    up = dot_plain(xn2, uw)
    act, gelu_back = jax.vjp(gelu_tanh, gate)
    hidden = (act * up).astype(jnp.bfloat16)
    ffn = tp_sum(dot_last(hidden, dw), n_tp, 2)
    funit, rf = norm_parts(ffn)
    block_output = h1 + funit * g_fo
    back_keys, back_values = (row_keys, row_values)
    dg_fo = jnp.sum(out_cotangent * funit, axis=0)
    dffn = norm_back(out_cotangent * g_fo, funit, rf).astype(jnp.bfloat16)
    dhid = dot_plain(dffn, dw)
    d_down = dot_first(dffn, hidden)
    dup = (dhid * act).astype(jnp.bfloat16)
    dgate = gelu_back(dhid * up)[0].astype(jnp.bfloat16)
    d_gate_w = dot_first(xn2, dgate)
    d_up_w = dot_first(xn2, dup)
    dxn2 = tp_sum(dot_last(dgate, gw) + dot_last(dup, uw), n_tp, 3)
    dg_fi = jnp.sum(dxn2 * unit2, axis=0)
    dh1 = out_cotangent + norm_back(dxn2 * g_fi, unit2, r2)
    dg_ao = jnp.sum(dh1 * aunit, axis=0)
    dproj = norm_back(dh1 * g_ao, aunit, ra).astype(jnp.bfloat16)
    d_o_w = dot_first(dproj, attended)
    dattended = dot_plain(dproj, ow).astype(jnp.bfloat16)
    win_keys, win_values, win_allowed = (back_keys, back_values, allowed)
    key_terms = jnp.zeros((row_len, HD), jnp.float32)
    value_terms = jnp.zeros((row_len, HD), jnp.float32)
    dq_parts = []
    for head in range(local_heads):
        query_head = queries[:, head, :]
        out_head = attended[:, head * HD : (head + 1) * HD]
        dout_head = dattended[:, head * HD : (head + 1) * HD]
        logits = masked_scores(query_head, win_keys, win_allowed, scaling)
        weights = jnp.exp(logits - lses[head])
        weights_low = weights.astype(jnp.bfloat16)
        delta = jnp.sum(
            dout_head.astype(jnp.float32) * out_head.astype(jnp.float32), axis=1, keepdims=True
        )
        dprob = dot_last(dout_head, win_values)
        dscore = (weights * (dprob - delta) * scaling).astype(jnp.bfloat16)
        dq_parts.append(dot_plain(dscore, win_keys))
        key_terms = key_terms + dot_first(dscore, query_head)
        value_terms = value_terms + dot_first(weights_low, dout_head)
    dq = jnp.stack(dq_parts, axis=1)
    dqn = unrotate(dq, cosine[:, None, :], sine[:, None, :])
    dg_q = jnp.sum(dqn * qunit, axis=(0, 1))
    dqp = norm_back(dqn * g_q, qunit, rq).reshape(tokens, local_heads * HD).astype(jnp.bfloat16)
    dkv = ctx_scatter(jnp.concatenate([key_terms, value_terms], axis=1), n_ctx, 4)
    dkn = unrotate(dkv[:, :HD], cosine, sine)
    dg_k = jnp.sum(dkn * kunit, axis=0)
    dkp = norm_back(dkn * g_k, kunit, rk).astype(jnp.bfloat16)
    dkvp = jnp.concatenate([dkp, dkv[:, HD:].astype(jnp.bfloat16)], axis=1)
    dxn1 = tp_sum(dot_last(dqp, qw) + dot_last(dkvp, kvw), n_tp, 5)
    d_q_w = dot_first(xn1, dqp)
    d_kv_w = dot_first(xn1, dkvp)
    dg_ai = jnp.sum(dxn1 * unit1, axis=0)
    input_grad = dh1 + norm_back(dxn1 * g_ai, unit1, r1)
    low = [
        item.astype(jnp.bfloat16) for item in (d_q_w, d_kv_w, d_o_w, d_gate_w, d_up_w, d_down)
    ]
    share = 1.0 / n_tp
    gain_terms = (dg_ai * share, dg_ao * share, dg_fi * share, dg_fo * share, dg_q, dg_k)
    q_out, k_out, o_out, gate_out, up_out, down_out, v_out, gain_sums = reduce_grads(
        n_shard, n_ctx, n_tp, low, 1, pack_lanes(gain_terms)
    )
    flat = gain_sums.reshape(-1)
    gain_outs = []
    at = 0
    for term in gain_terms:
        own = term.shape[0] // n_shard
        gain_outs.append(
            lax.dynamic_slice_in_dim(flat, at + lax.axis_index("shard") * own, own)
        )
        at = at + term.shape[0]
    return (
        block_output,
        input_grad,
        q_out,
        k_out,
        v_out,
        o_out,
        gate_out,
        up_out,
        down_out,
        *gain_outs,
    )


def solution(mesh):
    placed = (
        P(("shard", "ctx"), None),
        P(("shard", "ctx"), None),
        P("shard", None),
        P("shard", "tp"),
        P("shard", None),
        P("shard", None),
        P("shard", "tp"),
        P("shard", "tp"),
        P("shard", "tp"),
        P("shard", "tp"),
        P("shard"),
        P("shard"),
        P("shard"),
        P("shard"),
        P("shard"),
        P("shard"),
    )
    return jax.shard_map(
        per_device,
        mesh=mesh,
        in_specs=placed,
        out_specs=(
            P(("shard", "ctx"), None),
            P(("shard", "ctx"), None),
            P("shard", "tp"),
            P("shard", None),
            P("shard", None),
            P("shard", "tp"),
            P("shard", "tp"),
            P("shard", "tp"),
            P("shard", "tp"),
            P("shard"),
            P("shard"),
            P("shard"),
            P("shard"),
            P("shard"),
            P("shard"),
        ),
        check_vma=False,
    )
```

time: 789 us -> 243 us (0.31)
  waiting for transfers between devices: 568 us -> 0 us
  Pallas kernels: 0 us -> 163 us
  blocking collectives: 128 us -> 0 us
  between operations: 19.2 us -> 1.82 us
    reduce_scatter x9 -> x0, waiting for transfers between devices: 326 us -> none  [the longest x1 54.1 us: per_device(): lax.psum_scatter(d_up_w, 'shard', scatter_dimension=0, tiled=True)]
    psum x6 -> x0, waiting for transfers between devices: 172 us -> none  [the longest x1 61.9 us: per_device(): lax.psum((rows[0], rows[3], rows[4], rows[5], rows[6], rows[7], rows[8],...]
    pallas_call x0 -> x7, Pallas kernels: none -> 163 us  [the longest x1 73.9 us: reduce_grads(): pl.pallas_call(functools.partial(grad_kernel, n_shard, n_ctx, n_tp, count...]
    all_gather x6 -> x0, blocking collectives: 74.2 us -> none  [the longest x1 17 us: per_device(): lax.all_gather(q_weight, 'shard', axis=0, tiled=True)]
    all_gather x3 -> x0, waiting for transfers between devices: 68.2 us -> none  [the longest x1 30.5 us: per_device(): lax.all_gather(up_weight, 'shard', axis=0, tiled=True)]
    unnamed x2 -> x0, blocking collectives: 32.9 us -> none
    psum x2 -> x0, blocking collectives: 20.6 us -> none  [the longest x1 13 us: per_device(): lax.psum((rows[1], rows[2], rows[11], rows[12]), ('ctx', 'tp'))]
    unnamed x141 -> x163, local copies, waits for them, and re-layouts: 20.6 us -> 14 us
  transfers between devices with their start and end apart: 18 -> 0, of which waited for: 18 -> 0; matrix products, arithmetic and copies ran while one was open for 4% -> 0% of each run, Pallas kernels for 0% -> 0%
where the time goes in v1:
time: 243 us; the launch traced here: 241 us
  Pallas kernels  163 us (67%)
  other arithmetic  26.5 us (11%)
  local copies, waits for them, and re-layouts  26.2 us (11%)
  matrix products  23.9 us (10%)
    pallas_call x1, Pallas kernels, reduce_grads(): pl.pallas_call(functools.partial(grad_kernel, n_shard, n_ctx, n_tp, count...  73.9 us
    pallas_call x1, Pallas kernels, gather_all(): pl.pallas_call(functools.partial(gather_kernel, n_shard, n_ctx, count), o...  49 us
    pallas_call x4, Pallas kernels, tp_sum(): pl.pallas_call(functools.partial(tp_kernel, n_tp), out_shape=jax.ShapeDty...  30.9 us
    unnamed x163, local copies, waits for them, and re-layouts  14 us
    dot_general x10, matrix products, dot_first(): lax.dot_general(left, right, (((0,), (0,)), ((), ())), preferred_element_...  9.52 us
    pallas_call x1, Pallas kernels, ctx_scatter(): pl.pallas_call(functools.partial(ctx_kernel, n_ctx), out_shape=jax.ShapeD...  8.89 us
    dot_general x10, matrix products, dot_plain(): return jnp.dot(left, right, preferred_element_type=jnp.float32)  8.02 us
    dot_general x10, matrix products, dot_last(): lax.dot_general(left, right, (((1,), (1,)), ((), ())), preferred_element_...  6.38 us

profile of v1, /device:TPU:0, one launch (start us, length us, event | category | flops | bytes accessed | tf_op | source)
XLA Modules:
  0.0 241.1 jit_solution(9099586038078476142)
XLA Ops:
  0.6 1.6 pad_maximum_fusion.3.refs_1_
  3.4 1.7 multiply_convert_fusion.9.refs_6_
  5.1 4.1 %concatenate.38 = bf16[768]{0:T(1024)(128)(2,1)S(1)} concatenate(bf16[160]{0:T(256)(128)(2,1)} %param.26, bf16[160]{0:T(256)(128)(2,1)} %param.27, bf16[160]{0:T(256)(128)(2,1)} %param.28, bf16[160]{0:T(256)(128)(2,1)} %param.29, bf16[64]{0:T(256)(128)(2,1)} %param.30, bf16[64]{0:T(256)(128)(2,1)} %param.31), dimensions={0} | concatenate | bytes 3072 | tf_op jit(solution)/shard_map/concatenate | solution.py:510
  9.8 49.0 %gather_all.1 = (bf16[640,512]{1,0:T(8,128)(2,1)}, bf16[640,512]{1,0:T(8,128)(2,1)}, bf16[640,512]{1,0:T(8,128)(2,1)}, bf16[640,1024]{1,0:T(8,128)(2,1)}, bf16[6...) custom-call(bf16[160,512]{1,0:T(8,128)(2,1)} %refs_0_.1, ...), custom_call_target="tpu_custom_call" | custom-call | tf_op jit(solution)/shard_map/gather_all/pallas_call | solution.py:203
  60.4 1.9 fusion.12
  64.0 1.9 subtract_convert_fusion
  71.9 8.1 %tp_sum1.1 = f32[128,640]{1,0:T(8,128)} custom-call(bf16[128,640]{1,0:T(8,128)(2,1)} %convolution_convert_fusion.6.part), custom_call_target="tpu_custom_call" | custom-call | tf_op jit(solution)/shard_map/tp_sum1/pallas_call | solution.py:243
  81.2 1.7 multiply_reduce_fusion.10
  84.2 1.8 fusion.61
  86.0 1.2 multiply_convert_fusion.3
  88.0 1.2 convolution_convert_fusion.7.part
  89.2 7.3 %tp_sum2.1 = f32[128,640]{1,0:T(8,128)} custom-call(bf16[128,640]{1,0:T(8,128)(2,1)} %convolution_convert_fusion.7.part), custom_call_target="tpu_custom_call" | custom-call | tf_op jit(solution)/shard_map/tp_sum2/pallas_call | solution.py:243
  98.9 2.0 multiply_reduce_fusion.1
  100.9 1.9 multiply_convert_fusion.5
  102.8 1.8 multiply_convert_fusion.2
  105.3 1.2 fusion.9.part
  106.5 7.0 %tp_sum3.1 = f32[128,640]{1,0:T(8,128)} custom-call(bf16[128,640]{1,0:T(8,128)(2,1)} %fusion.9.part), custom_call_target="tpu_custom_call" | custom-call | tf_op jit(solution)/shard_map/tp_sum3/pallas_call | solution.py:243
  114.8 1.3 multiply_reduce_fusion.3
  122.7 8.9 %ctx_scatter4.1 = f32[128,512]{1,0:T(8,128)} custom-call(bf16[512,512]{1,0:T(8,128)(2,1)} %pad_maximum_fusion.part), custom_call_target="tpu_custom_call" | custom-call | tf_op jit(solution)/shard_map/ctx_scatter4/pallas_call | solution.py:285
  135.4 8.4 %tp_sum5.1 = f32[128,640]{1,0:T(8,128)} custom-call(bf16[128,640]{1,0:T(8,128)(2,1)} %fusion.8.part), custom_call_target="tpu_custom_call" | custom-call | tf_op jit(solution)/shard_map/tp_sum5/pallas_call | solution.py:243
  145.1 1.9 multiply_add_fusion
  146.9 1.2 convolution_convert_fusion.5.refs_0_
  149.3 1.2 convolution_convert_fusion.3.refs_2_
  150.5 1.6 convolution_convert_fusion.2.refs_3_
  152.1 1.6 convolution_convert_fusion.1.refs_4_
  153.7 1.6 convolution_convert_fusion.refs_5_
  156.0 73.9 %reduce_grads.1 = (f32[160,512]{1,0:T(8,128)}, f32[160,256]{1,0:T(8,128)}, f32[160,512]{1,0:T(8,128)}, f32[160,1024]{1,0:T(8,128)}, f32[160,1024]{1,0:T(8,128)},...) custom-call(bf16[640,512]{1,0:T(8,128)(2,1)} %convolution_convert_fusion.5.refs_0_, ...), custom_call_target="tpu_custom_call" | custom-call | tf_op jit(solution)/shard_map/reduce_grads/pallas_call | solution.py:471
  230.0 1.5 fusion.53
  231.5 1.3 fusion.52
  232.8 1.7 copy.113
  234.6 1.7 copy.114
  236.2 1.6 copy.115
  (249 shorter events, 34.4 us)
Async XLA Ops:
  3.3 62.6 %copy-start.63 = (f32[128]{0:T(128)}, f32[128]{0:T(128)S(1)}, u32[]{:S(2)}) copy-start(f32[128]{0:T(128)S(1)} %add_rsqrt_fusion.5) | copy-start | bytes 1540
  60.4 2.4 %copy-start.59 = (f32[256]{0:T(256)}, f32[256]{0:T(256)S(1)}, u32[]{:S(2)}) copy-start(f32[256]{0:T(256)S(1)} %mul.559) | copy-start | bytes 3076
  62.8 3.1 %copy-start.62 = (f32[512]{0:T(512)}, f32[512]{0:T(512)S(1)}, u32[]{:S(2)}) copy-start(f32[512]{0:T(512)S(1)} %add_rsqrt_fusion) | copy-start | bytes 6148
  62.8 3.1 %copy-start = (f32[128,640]{1,0:T(8,128)S(1)}, f32[128,640]{1,0:T(8,128)}, u32[]{:S(2)}) copy-start(f32[128,640]{1,0:T(8,128)} %param.16) | copy-start | bytes 983044
  63.7 2.3 copy-start.10
  65.9 3.0 %copy-start.50 = (bf16[512,128]{1,0:T(8,128)(2,1)}, bf16[512,128]{1,0:T(8,128)(2,1)S(1)}, u32[]{:S(2)}) copy-start(bf16[512,128]{1,0:T(8,128)(2,1)S(1)} %get-tuple-element.70) | copy-start | bytes 393220
  66.4 2.0 copy-start.56
  68.4 1.9 copy-start.4
  68.6 2.3 copy-start.12
  82.9 3.1 %copy-start.2 = (bf16[640,1024]{1,0:T(8,128)(2,1)S(1)}, bf16[640,1024]{1,0:T(8,128)(2,1)}, u32[]{:S(2)}) copy-start(bf16[640,1024]{1,0:T(8,128)(2,1)} %get-tuple-element.37) | copy-start | bytes 3932164
  84.2 3.0 %copy-start.6 = (bf16[128,640]{1,0:T(8,128)(2,1)}, bf16[128,640]{1,0:T(8,128)(2,1)S(1)}, u32[]{:S(2)}) copy-start(bf16[128,640]{1,0:T(8,128)(2,1)S(1)} %multiply_convert_fusion.6) | copy-start | bytes 491524
  86.0 1.9 copy-start.20
  98.9 4.0 %copy-start.19 = (f32[128,1024]{1,0:T(8,128)S(1)}, f32[128,1024]{1,0:T(8,128)}, u32[]{:S(2)}) copy-start(f32[128,1024]{1,0:T(8,128)} %copy-done.18) | copy-start | bytes 1572868
  98.9 4.0 %copy-start.21 = (bf16[640,1024]{1,0:T(8,128)(2,1)S(1)}, bf16[640,1024]{1,0:T(8,128)(2,1)}, u32[]{:S(2)}) copy-start(bf16[640,1024]{1,0:T(8,128)(2,1)} %get-tuple-element.38) | copy-start | bytes 3932164
  105.2 8.3 %copy-start.68 = (f32[128]{0:T(128)S(1)}, f32[128]{0:T(128)}, u32[]{:S(2)}) copy-start(f32[128]{0:T(128)} %copy-done.67) | copy-start | bytes 1540
  105.2 9.5 %copy-start.1 = (f32[128,640]{1,0:T(8,128)S(1)}, f32[128,640]{1,0:T(8,128)}, u32[]{:S(2)}) copy-start(f32[128,640]{1,0:T(8,128)} %tp_sum1.1) | copy-start | bytes 983044
  105.2 9.5 %copy-start.8 = (f32[128,640]{1,0:T(8,128)S(1)}, f32[128,640]{1,0:T(8,128)}, u32[]{:S(2)}) copy-start(f32[128,640]{1,0:T(8,128)} %param.17) | copy-start | bytes 983044
  105.2 9.5 %copy-start.66 = (f32[128]{0:T(128)S(1)}, f32[128]{0:T(128)}, u32[]{:S(2)}) copy-start(f32[128]{0:T(128)} %copy-done.65) | copy-start | bytes 1540
  121.8 11.6 %copy-start.22 = (f32[512,256]{1,0:T(8,128)S(1)}, f32[512,256]{1,0:T(8,128)}, u32[]{:S(2)}) copy-start(f32[512,256]{1,0:T(8,128)} %get-tuple-element.65) | copy-start | bytes 1572868
  121.8 11.6 %copy-start.60 = (f32[256]{0:T(256)S(1)}, f32[256]{0:T(256)}, u32[]{:S(2)}) copy-start(f32[256]{0:T(256)} %copy-done.59) | copy-start | bytes 3076
  121.8 12.6 %copy-start.9 = (bf16[640,512]{1,0:T(8,128)(2,1)S(1)}, bf16[640,512]{1,0:T(8,128)(2,1)}, u32[]{:S(2)}) copy-start(bf16[640,512]{1,0:T(8,128)(2,1)} %get-tuple-element.34) | copy-start | bytes 1966084
  132.5 11.4 %copy-start.64 = (f32[128]{0:T(128)S(1)}, f32[128]{0:T(128)}, u32[]{:S(2)}) copy-start(f32[128]{0:T(128)} %copy-done.63) | copy-start | bytes 1540
  135.4 11.5 %copy-start.15 = (bf16[128,640]{1,0:T(8,128)(2,1)S(1)}, bf16[128,640]{1,0:T(8,128)(2,1)}, u32[]{:S(2)}) copy-start(bf16[128,640]{1,0:T(8,128)(2,1)} %copy-done.14) | copy-start | bytes 491524
  145.1 4.3 %copy-start.35 = (bf16[128,256]{1,0:T(8,128)(2,1)S(1)}, bf16[128,256]{1,0:T(8,128)(2,1)}, u32[]{:S(2)}) copy-start(bf16[128,256]{1,0:T(8,128)(2,1)} %copy-done.33) | copy-start | bytes 196612
  146.9 3.6 %copy-start.7 = (bf16[128,640]{1,0:T(8,128)(2,1)S(1)}, bf16[128,640]{1,0:T(8,128)(2,1)}, u32[]{:S(2)}) copy-start(bf16[128,640]{1,0:T(8,128)(2,1)} %copy-done.6) | copy-start | bytes 491524
  146.9 3.6 %copy-start.30 = (bf16[128,1024]{1,0:T(8,128)(2,1)S(1)}, bf16[128,1024]{1,0:T(8,128)(2,1)}, u32[]{:S(2)}) copy-start(bf16[128,1024]{1,0:T(8,128)(2,1)} %copy-done.29) | copy-start | bytes 786436
  149.3 2.8 %copy-start.28 = (bf16[128,1024]{1,0:T(8,128)(2,1)S(1)}, bf16[128,1024]{1,0:T(8,128)(2,1)}, u32[]{:S(2)}) copy-start(bf16[128,1024]{1,0:T(8,128)(2,1)} %copy-done.27) | copy-start | bytes 786436
  150.5 3.2 %copy-start.17 = (bf16[128,1024]{1,0:T(8,128)(2,1)S(1)}, bf16[128,1024]{1,0:T(8,128)(2,1)}, u32[]{:S(2)}) copy-start(bf16[128,1024]{1,0:T(8,128)(2,1)} %copy-done.16) | copy-start | bytes 786436
  150.5 3.2 %copy-start.40 = (bf16[128,640]{1,0:T(8,128)(2,1)S(1)}, bf16[128,640]{1,0:T(8,128)(2,1)}, u32[]{:S(2)}) copy-start(bf16[128,640]{1,0:T(8,128)(2,1)} %copy-done.39) | copy-start | bytes 491524
  230.0 7.8 %copy-start.49 = (f32[160,512]{1,0:T(8,128)S(1)}, f32[160,512]{1,0:T(8,128)}, u32[]{:S(2)}) copy-start(f32[160,512]{1,0:T(8,128)} %get-tuple-element.124) | copy-start | bytes 983044
  230.0 8.6 %copy-start.38 = (f32[160,1024]{1,0:T(8,128)S(1)}, f32[160,1024]{1,0:T(8,128)}, u32[]{:S(2)}) copy-start(f32[160,1024]{1,0:T(8,128)} %get-tuple-element.125) | copy-start | bytes 1966084
  234.6 4.8 %copy-start.37 = (f32[160,1024]{1,0:T(8,128)S(1)}, f32[160,1024]{1,0:T(8,128)}, u32[]{:S(2)}) copy-start(f32[160,1024]{1,0:T(8,128)} %get-tuple-element.126) | copy-start | bytes 1966084
  (42 other events, 52.6 us)

commit v2 on v1

--- a/solution.py
+++ b/solution.py
@@ -255,59 +255,37 @@
     )(part)
 
 
-def ctx_kernel(n_ctx, part, out, inbox, send_sem, recv_sem):
-    shard, ctx, tp = (lax.axis_index("shard"), lax.axis_index("ctx"), lax.axis_index("tp"))
-    tokens = out.shape[0]
-    peers = [(shard, lax.rem(ctx + d, n_ctx), tp) for d in range(1, n_ctx)]
-    greet(peers)
-    copies = [
-        send(
-            part.at[block_rows(peers[d - 1][1], tokens)],
-            inbox.at[d - 1],
-            (send_sem, recv_sem),
-            d - 1,
-            peers[d - 1],
-        )
-        for d in range(1, n_ctx)
-    ]
-    total = part[block_rows(ctx, tokens), :].astype(jnp.float32)
-    for d in range(1, n_ctx):
-        copies[d - 1].wait_recv()
-        total = total + inbox[d - 1].astype(jnp.float32)
-    out[...] = total
-    for copy in copies:
-        copy.wait_send()
-
-
-def ctx_scatter(value, n_ctx, number):
-    part = value.astype(jnp.bfloat16)
-    piece = (part.shape[0] // n_ctx, part.shape[1])
-    return pl.pallas_call(
-        functools.partial(ctx_kernel, n_ctx),
-        out_shape=jax.ShapeDtypeStruct(piece, jnp.float32),
-        in_specs=[vmem()],
-        out_specs=vmem(),
-        scratch_shapes=[
-            pltpu.VMEM((n_ctx - 1,) + piece, jnp.bfloat16),
-            pltpu.SemaphoreType.DMA((n_ctx - 1,)),
-            pltpu.SemaphoreType.DMA((n_ctx - 1,)),
-        ],
-        compiler_params=params(number),
-        name=f"ctx_scatter{number}",
-    )(part)
-
-
-def grad_kernel(n_shard, n_ctx, n_tp, count, kv_at, *refs):
-    grads, gain = (refs[:count], refs[count])
-    refs = refs[count + 1 :]
-    outs, gain_out = (refs[: count + 1], refs[count + 1])
+def tail_kernel(n_shard, n_ctx, n_tp, early, *refs):
+    ready = refs[:early]
+    (terms, dqp, qw, kvw, xn1_t, cosine, sine, kunit, rk, g_k, unit1, r1, g_ai, dh1, gain) = refs[
+        early : early + 15
+    ]
+    refs = refs[early + 15 :]
+    count = early + 2
+    kv_at = count - 1
+    outs, gain_out, input_grad = (refs[: count + 1], refs[count + 1], refs[count + 2])
+    (late_q, late_kv, dkv_in, part, part_in) = refs[count + 3 : count + 8]
     (half, away, inbox, mine, arrived, done, kv_in, groups_in, shared) = refs[
-        count + 2 : count + 11
-    ]
-    (g_near, g_far, g_mid, g_shard, g_group, g_tp) = refs[count + 11 : count + 17]
-    sems = refs[count + 17 :]
+        count + 8 : count + 17
+    ]
+    (g_own, g_near, g_far, g_mid, g_shard, g_group, g_tp) = refs[count + 17 : count + 24]
+    sems = refs[count + 24 :]
     pair = [(sems[2 * k], sems[2 * k + 1]) for k in range(len(sems) // 2)]
-    s_core, s_far, s_shard, s_group, s_kv, s_share, s_gain, s_gz, s_gg, s_gt = pair
+    (
+        s_core,
+        s_far,
+        s_shard,
+        s_group,
+        s_kv,
+        s_share,
+        s_gain,
+        s_gz,
+        s_gg,
+        s_gt,
+        s_dkv,
+        s_part,
+    ) = pair
+    grads = list(ready) + [late_q, late_kv]
     shard, ctx, tp, near, far = place(n_ctx)
     n_groups = n_ctx // WAYS
     group = lax.div(ctx, WAYS)
@@ -315,91 +293,171 @@
     beside = lax.rem(near, WAYS)
     opposite = beside + other - member
     rows = outs[0].shape[0]
+    tokens = dqp.shape[0]
     widths = [item.shape[1] // WAYS for item in grads]
     starts = [sum(widths[:a]) for a in range(count)]
+    batches = (list(range(early)), [early, early + 1])
+    spans = (
+        pl.ds(0, starts[early]),
+        pl.ds(starts[early], widths[early] + widths[early + 1]),
+    )
     near_id, far_id = ((shard, near, tp), (shard, far, tp))
     z_ids = [(lax.rem(shard + d, n_shard), ctx, tp) for d in range(1, n_shard)]
+    c_ids = [(shard, lax.rem(ctx + d, n_ctx), tp) for d in range(1, n_ctx)]
     g_ids = [(shard, lax.rem(ctx + WAYS * d, n_ctx), tp) for d in range(1, n_groups)]
     t_ids = [(shard, ctx, lax.rem(tp + d, n_tp)) for d in range(1, n_tp)]
-    greet([near_id, far_id] + z_ids + g_ids + t_ids)
+    greet(z_ids + c_ids + t_ids)
 
     ends = []
     core = {}
-    for slot, quarter in ((1, opposite), (0, beside)):
-        for a in range(count):
-            core[slot, a] = send(
-                grads[a].at[:, columns(quarter, widths[a])],
-                half.at[slot, :, pl.ds(starts[a], widths[a])],
-                s_core,
-                (slot, a),
-                near_id,
-            )
-    gain_near = send(gain, g_near, s_gain, 0, near_id)
+    over = {}
+    along = {}
     order = list(range(1, n_shard)) + [0]
     targets = [lax.rem(shard + d, n_shard) for d in range(n_shard)]
 
-    for a in range(count):
-        core[1, a].wait_recv()
-    over = {}
-    for d in order:
-        where = block_rows(targets[d], rows)
-        for a in range(count):
-            cols = pl.ds(starts[a], widths[a])
-            total = half[1, where, cols].astype(jnp.float32) + grads[a][
-                where, columns(other, widths[a])
-            ].astype(jnp.float32)
-            away[where, cols] = total.astype(jnp.bfloat16)
-        over[d] = send(away.at[where], inbox.at[where], s_far, d, far_id)
-
+    def start_core(batch):
+        for slot, quarter in ((1, opposite), (0, beside)):
+            for a in batches[batch]:
+                core[slot, a] = send(
+                    grads[a].at[:, columns(quarter, widths[a])],
+                    half.at[slot, :, pl.ds(starts[a], widths[a])],
+                    s_core,
+                    (slot, a),
+                    near_id,
+                )
+
+    def start_over(batch):
+        for a in batches[batch]:
+            core[1, a].wait_recv()
+        for d in order:
+            where = block_rows(targets[d], rows)
+            for a in batches[batch]:
+                cols = pl.ds(starts[a], widths[a])
+                total = half[1, where, cols].astype(jnp.float32) + grads[a][
+                    where, columns(other, widths[a])
+                ].astype(jnp.float32)
+                away[where, cols] = total.astype(jnp.bfloat16)
+            over[batch, d] = send(
+                away.at[where, spans[batch]],
+                inbox.at[where, spans[batch]],
+                s_far,
+                (batch, d),
+                far_id,
+            )
+
+    def start_along(batch):
+        for a in batches[batch]:
+            core[0, a].wait_recv()
+        for d in order:
+            where = block_rows(targets[d], rows)
+            over[batch, d].wait_recv()
+            for a in batches[batch]:
+                cols = pl.ds(starts[a], widths[a])
+                total = (
+                    half[0, where, cols].astype(jnp.float32)
+                    + grads[a][where, columns(member, widths[a])].astype(jnp.float32)
+                    + inbox[where, cols].astype(jnp.float32)
+                )
+                mine[where, cols] = total.astype(jnp.bfloat16)
+            if d:
+                along[batch, d] = send(
+                    mine.at[where, spans[batch]],
+                    arrived.at[d - 1, :, spans[batch]],
+                    s_shard,
+                    (batch, d - 1),
+                    z_ids[d - 1],
+                )
+
+    def finish(batch):
+        span = spans[batch]
+        total = mine[block_rows(shard, rows), span].astype(jnp.float32)
+        for d in range(1, n_shard):
+            along[batch, d].wait_recv()
+            total = total + arrived[d - 1, :, span].astype(jnp.float32)
+        if n_groups > 1:
+            groups_in[group, :, span] = total.astype(jnp.bfloat16)
+            piece = groups_in.at[group, :, span]
+            moved = [
+                send(piece, piece, s_group, (batch, d - 1), g_ids[d - 1])
+                for d in range(1, n_groups)
+            ]
+            for item in moved:
+                item.wait_recv()
+            ends.extend(moved)
+            total = groups_in[0, :, span].astype(jnp.float32)
+            for g in range(1, n_groups):
+                total = total + groups_in[g, :, span].astype(jnp.float32)
+        return total.astype(jnp.bfloat16)
+
+    def start_share(batch):
+        piece = shared.at[member, :, spans[batch]]
+        return (
+            send(piece, piece, s_share, (batch, 0), far_id),
+            send(piece, piece, s_share, (batch, 1), near_id),
+        )
+
+    def relay_share(batch, first):
+        first[0].wait_recv()
+        piece = shared.at[other, :, spans[batch]]
+        return send(piece, piece, s_share, (batch, 2), near_id)
+
+    scatter = [
+        send(
+            terms.at[block_rows(c_ids[d - 1][1], tokens)],
+            dkv_in.at[d - 1],
+            s_dkv,
+            d - 1,
+            c_ids[d - 1],
+        )
+        for d in range(1, n_ctx)
+    ]
+    start_core(0)
+    late_q[...] = dot_plain(xn1_t[...], dqp[...]).astype(jnp.bfloat16)
+    dxn1 = dot_last(dqp[...], qw[...])
+    dkv = terms[block_rows(ctx, tokens), :].astype(jnp.float32)
+    for d in range(1, n_ctx):
+        scatter[d - 1].wait_recv()
+        dkv = dkv + dkv_in[d - 1].astype(jnp.float32)
+    dkn = unrotate(dkv[:, :HD], cosine[...], sine[...])
+    dg_k = jnp.sum(dkn * kunit[...], axis=0, keepdims=True)
+    dkp = norm_back(dkn * g_k[...], kunit[...], rk[...]).astype(jnp.bfloat16)
+    dkvp = jnp.concatenate([dkp, dkv[:, HD:].astype(jnp.bfloat16)], axis=1)
+    part[...] = (dxn1 + dot_last(dkvp, kvw[...])).astype(jnp.bfloat16)
+    parts = [
+        send(part, part_in.at[d - 1], s_part, d - 1, t_ids[d - 1]) for d in range(1, n_tp)
+    ]
+    late_kv[...] = dot_plain(xn1_t[...], dkvp).astype(jnp.bfloat16)
+    start_over(0)
+    start_core(1)
+    dxn1 = part[...].astype(jnp.float32)
+    for d in range(1, n_tp):
+        parts[d - 1].wait_recv()
+        dxn1 = dxn1 + part_in[d - 1].astype(jnp.float32)
+    dg_ai = jnp.sum(dxn1 * unit1[...], axis=0, keepdims=True) * (1.0 / n_tp)
+    input_grad[...] = dh1[...] + norm_back(dxn1 * g_ai[...], unit1[...], r1[...])
+    g_own[...] = gain[...]
+    at = 0
+    for line in (dg_ai, dg_k):
+        for k in range(line.shape[1] // LANES):
+            g_own[pl.ds(at, 1), :] = line[:, k * LANES : (k + 1) * LANES]
+            at = at + 1
+    gain_near = send(g_own, g_near, s_gain, 0, near_id)
+    start_over(1)
     gain_near.wait_recv()
-    g_mid[0] = gain[...] + g_near[...]
+    g_mid[0] = g_own[...] + g_near[...]
     gain_far = send(g_mid.at[0], g_far, s_gain, 1, far_id)
 
-    for a in range(count):
-        core[0, a].wait_recv()
-    along = {}
-    for d in order:
-        where = block_rows(targets[d], rows)
-        over[d].wait_recv()
-        for a in range(count):
-            cols = pl.ds(starts[a], widths[a])
-            total = (
-                half[0, where, cols].astype(jnp.float32)
-                + grads[a][where, columns(member, widths[a])].astype(jnp.float32)
-                + inbox[where, cols].astype(jnp.float32)
-            )
-            mine[where, cols] = total.astype(jnp.bfloat16)
-        if d:
-            along[d] = send(mine.at[where], arrived.at[d - 1], s_shard, d - 1, z_ids[d - 1])
-
+    start_along(0)
     gain_far.wait_recv()
     g_shard[shard] = g_mid[0] + g_far[...]
     gz = [
         send(g_shard.at[shard], g_shard.at[shard], s_gz, d - 1, z_ids[d - 1])
         for d in range(1, n_shard)
     ]
-    total = mine[block_rows(shard, rows), :].astype(jnp.float32)
-    for d in range(1, n_shard):
-        along[d].wait_recv()
-        total = total + arrived[d - 1].astype(jnp.float32)
-    if n_groups > 1:
-        groups_in[group] = total.astype(jnp.bfloat16)
-        moved = [
-            send(groups_in.at[group], groups_in.at[group], s_group, d - 1, g_ids[d - 1])
-            for d in range(1, n_groups)
-        ]
-        for item in moved:
-            item.wait_recv()
-        ends = ends + moved
-        total = groups_in[0].astype(jnp.float32)
-        for g in range(1, n_groups):
-            total = total + groups_in[g].astype(jnp.float32)
-    done[...] = total.astype(jnp.bfloat16)
-    kv_cols = pl.ds(starts[kv_at], widths[kv_at])
-    kvs = [
-        send(done.at[:, kv_cols], kv_in.at[d - 1], s_kv, d - 1, t_ids[d - 1])
-        for d in range(1, n_tp)
-    ]
+    start_along(1)
+    shared[member, :, spans[0]] = finish(0)
+    share0 = start_share(0)
+
     for item in gz:
         item.wait_recv()
     total = g_shard[0]
@@ -420,70 +478,89 @@
         send(g_tp.at[tp], g_tp.at[tp], s_gt, d - 1, t_ids[d - 1]) for d in range(1, n_tp)
     ]
 
-    shared[member] = done[...]
+    done[...] = finish(1)
+    kv_cols = pl.ds(widths[early], widths[kv_at])
+    kvs = [
+        send(done.at[:, kv_cols], kv_in.at[d - 1], s_kv, d - 1, t_ids[d - 1])
+        for d in range(1, n_tp)
+    ]
+    relay0 = relay_share(0, share0)
+    shared[member, :, pl.ds(starts[early], widths[early])] = done[:, pl.ds(0, widths[early])]
     total = done[:, kv_cols].astype(jnp.float32)
     for d in range(1, n_tp):
         kvs[d - 1].wait_recv()
         total = total + kv_in[d - 1].astype(jnp.float32)
-    shared[member, :, kv_cols] = total.astype(jnp.bfloat16)
-    piece = shared.at[member]
-    to_far = send(piece, piece, s_share, 0, far_id)
-    to_near = send(piece, piece, s_share, 1, near_id)
-    to_far.wait_recv()
-    piece = shared.at[other]
-    relay = send(piece, piece, s_share, 2, near_id)
+    shared[member, :, pl.ds(starts[kv_at], widths[kv_at])] = total.astype(jnp.bfloat16)
+    share1 = start_share(1)
     for item in gt:
         item.wait_recv()
     total = g_tp[0]
     for k in range(1, n_tp):
         total = total + g_tp[k]
     gain_out[...] = total
-    to_near.wait_recv()
-    relay.wait_recv()
-    for q in range(WAYS):
-        for a in range(count):
-            value = shared[q, :, pl.ds(starts[a], widths[a])].astype(jnp.float32)
-            if a == kv_at:
-                out = outs[a] if q < WAYS // 2 else outs[count]
-                out[:, pl.ds((q % (WAYS // 2)) * widths[a], widths[a])] = value
-            else:
-                outs[a][:, pl.ds(q * widths[a], widths[a])] = value
-    ends = ends + list(core.values()) + [gain_near, gain_far, to_far, to_near, relay]
-    ends = ends + list(over.values()) + list(along.values()) + kvs + gz + gg + gt
+
+    def write(batch):
+        for q in range(WAYS):
+            for a in batches[batch]:
+                value = shared[q, :, pl.ds(starts[a], widths[a])]
+                if a == kv_at:
+                    out = outs[a] if q < WAYS // 2 else outs[count]
+                    out[:, pl.ds((q % (WAYS // 2)) * widths[a], widths[a])] = value
+                else:
+                    outs[a][:, pl.ds(q * widths[a], widths[a])] = value
+
+    share0[1].wait_recv()
+    relay0.wait_recv()
+    write(0)
+    relay1 = relay_share(1, share1)
+    share1[1].wait_recv()
+    relay1.wait_recv()
+    write(1)
+    ends.extend(scatter + parts + list(core.values()) + list(over.values()))
+    ends.extend(list(along.values()) + kvs + gz + gg + gt + [gain_near, gain_far])
+    ends.extend(list(share0) + list(share1) + [relay0, relay1])
     for item in ends:
         item.wait_send()
 
 
-def reduce_grads(n_shard, n_ctx, n_tp, grads, kv_at, gain):
-    count = len(grads)
-    deep = grads[0].shape[0]
+def run_tail(n_shard, n_ctx, n_tp, ready, terms, dqp, qw, kvw, xn1_t, small, dh1, gain):
+    deep = qw.shape[0]
+    tokens = dqp.shape[0]
     rows = deep // n_shard
     n_groups = n_ctx // WAYS
-    wide = sum([item.shape[1] // WAYS for item in grads])
-    out_widths = [item.shape[1] for item in grads]
-    out_widths[kv_at] = out_widths[kv_at] // 2
-    out_widths.append(out_widths[kv_at])
+    early = len(ready)
+    count = early + 2
+    late = (qw.shape[1], kvw.shape[1])
+    wide = sum([item.shape[1] // WAYS for item in ready]) + sum(late) // WAYS
+    out_widths = [item.shape[1] for item in ready] + [late[0], late[1] // 2, late[1] // 2]
     low, full = (jnp.bfloat16, jnp.float32)
+    operands = (*ready, terms, dqp, qw, kvw, xn1_t, *small, dh1, gain)
 
     def dma(*shape):
         return [pltpu.SemaphoreType.DMA(shape)] * 2
 
     return pl.pallas_call(
-        functools.partial(grad_kernel, n_shard, n_ctx, n_tp, count, kv_at),
-        out_shape=[jax.ShapeDtypeStruct((rows, item), full) for item in out_widths]
-        + [jax.ShapeDtypeStruct(gain.shape, full)],
-        in_specs=[vmem()] * (count + 1),
-        out_specs=[vmem()] * (count + 2),
+        functools.partial(tail_kernel, n_shard, n_ctx, n_tp, early),
+        out_shape=[jax.ShapeDtypeStruct((rows, item), low) for item in out_widths]
+        + [jax.ShapeDtypeStruct(gain.shape, full), jax.ShapeDtypeStruct(dh1.shape, full)],
+        in_specs=[vmem()] * len(operands),
+        out_specs=[vmem()] * (count + 3),
         scratch_shapes=[
+            pltpu.VMEM((deep, late[0]), low),
+            pltpu.VMEM((deep, late[1]), low),
+            pltpu.VMEM((n_ctx - 1, tokens, terms.shape[1]), low),
+            pltpu.VMEM((tokens, deep), low),
+            pltpu.VMEM((n_tp - 1, tokens, deep), low),
             pltpu.VMEM((2, deep, wide), low),
             pltpu.VMEM((deep, wide), low),
             pltpu.VMEM((deep, wide), low),
             pltpu.VMEM((deep, wide), low),
             pltpu.VMEM((n_shard - 1, rows, wide), low),
-            pltpu.VMEM((rows, wide), low),
-            pltpu.VMEM((n_tp - 1, rows, grads[kv_at].shape[1] // WAYS), low),
+            pltpu.VMEM((rows, sum(late) // WAYS), low),
+            pltpu.VMEM((n_tp - 1, rows, late[1] // WAYS), low),
             pltpu.VMEM((n_groups, rows, wide), low),
             pltpu.VMEM((WAYS, rows, wide), low),
+            pltpu.VMEM(gain.shape, full),
             pltpu.VMEM(gain.shape, full),
             pltpu.VMEM(gain.shape, full),
             pltpu.VMEM((1,) + gain.shape, full),
@@ -492,18 +569,20 @@
             pltpu.VMEM((n_tp,) + gain.shape, full),
         ]
         + dma(2, count)
-        + dma(n_shard)
+        + dma(2, n_shard)
+        + dma(2, n_shard - 1)
+        + dma(2, max(n_groups - 1, 1))
+        + dma(n_tp - 1)
+        + dma(2, 3)
+        + dma(2)
         + dma(n_shard - 1)
         + dma(max(n_groups - 1, 1))
         + dma(n_tp - 1)
-        + dma(3)
-        + dma(2)
-        + dma(n_shard - 1)
-        + dma(max(n_groups - 1, 1))
+        + dma(n_ctx - 1)
         + dma(n_tp - 1),
         compiler_params=params(6),
-        name="reduce_grads",
-    )(*grads, gain)
+        name="tail",
+    )(*operands)
 
 
 def pack_lanes(items):
@@ -645,33 +724,39 @@
     dqn = unrotate(dq, cosine[:, None, :], sine[:, None, :])
     dg_q = jnp.sum(dqn * qunit, axis=(0, 1))
     dqp = norm_back(dqn * g_q, qunit, rq).reshape(tokens, local_heads * HD).astype(jnp.bfloat16)
-    dkv = ctx_scatter(jnp.concatenate([key_terms, value_terms], axis=1), n_ctx, 4)
-    dkn = unrotate(dkv[:, :HD], cosine, sine)
-    dg_k = jnp.sum(dkn * kunit, axis=0)
-    dkp = norm_back(dkn * g_k, kunit, rk).astype(jnp.bfloat16)
-    dkvp = jnp.concatenate([dkp, dkv[:, HD:].astype(jnp.bfloat16)], axis=1)
-    dxn1 = tp_sum(dot_last(dqp, qw) + dot_last(dkvp, kvw), n_tp, 5)
-    d_q_w = dot_first(xn1, dqp)
-    d_kv_w = dot_first(xn1, dkvp)
-    dg_ai = jnp.sum(dxn1 * unit1, axis=0)
-    input_grad = dh1 + norm_back(dxn1 * g_ai, unit1, r1)
-    low = [
-        item.astype(jnp.bfloat16) for item in (d_q_w, d_kv_w, d_o_w, d_gate_w, d_up_w, d_down)
-    ]
+    terms = jnp.concatenate([key_terms, value_terms], axis=1).astype(jnp.bfloat16)
+    ready = [item.astype(jnp.bfloat16) for item in (d_o_w, d_gate_w, d_up_w, d_down)]
     share = 1.0 / n_tp
-    gain_terms = (dg_ai * share, dg_ao * share, dg_fi * share, dg_fo * share, dg_q, dg_k)
-    q_out, k_out, o_out, gate_out, up_out, down_out, v_out, gain_sums = reduce_grads(
-        n_shard, n_ctx, n_tp, low, 1, pack_lanes(gain_terms)
-    )
+    late = (jnp.zeros((width,), jnp.float32), jnp.zeros((HD,), jnp.float32))
+    sums = (*late, dg_ao * share, dg_fi * share, dg_fo * share, dg_q)
+    outs = run_tail(
+        n_shard,
+        n_ctx,
+        n_tp,
+        ready,
+        terms,
+        dqp,
+        qw,
+        kvw,
+        xn1.T,
+        (cosine, sine, kunit, rk, g_k[None, :], unit1, r1, g_ai[None, :]),
+        dh1,
+        pack_lanes(sums),
+    )
+    o_out, gate_out, up_out, down_out, q_out, k_out, v_out = [
+        item.astype(jnp.float32) for item in outs[:7]
+    ]
+    gain_sums, input_grad = outs[7:]
     flat = gain_sums.reshape(-1)
     gain_outs = []
     at = 0
-    for term in gain_terms:
+    for term in sums:
         own = term.shape[0] // n_shard
         gain_outs.append(
             lax.dynamic_slice_in_dim(flat, at + lax.axis_index("shard") * own, own)
         )
         at = at + term.shape[0]
+    dg_ai, dg_k, dg_ao, dg_fi, dg_fo, dg_q = gain_outs
     return (
         block_output,
         input_grad,
@@ -682,7 +767,12 @@
         gate_out,
         up_out,
         down_out,
-        *gain_outs,
+        dg_ai,
+        dg_ao,
+        dg_fi,
+        dg_fo,
+        dg_q,
+        dg_k,
     )
 
 

time: 243 us -> 215 us (0.88)
  Pallas kernels: 163 us -> 142 us
  local copies, waits for them, and re-layouts: 26.2 us -> 18.1 us
  other arithmetic: 26.5 us -> 32.6 us
  matrix products: 23.9 us -> 20.2 us
    pallas_call x2 -> x1, Pallas kernels: 82.8 us -> 70.4 us  [run_tail(): pl.pallas_call(functools.partial(tail_kernel, n_shard, n_ctx, n_tp, early...]
    unnamed x163 -> x140, local copies, waits for them, and re-layouts: 14 us -> 4.31 us
    convert_element_type x2 -> x7, other arithmetic: 0.2 us -> 9.29 us  [per_device(): item.astype(jnp.float32)]
    pallas_call x4 -> x3, Pallas kernels: 30.9 us -> 22.5 us  [tp_sum(): pl.pallas_call(functools.partial(tp_kernel, n_tp), out_shape=jax.ShapeDty...]
    concatenate x2, local copies, waits for them, and re-layouts: 4.09 us -> 0.1 us  [pack_lanes(): flat = jnp.concatenate([item.astype(jnp.float32) for item in items])]
    dynamic_slice x0 -> x3, local copies, waits for them, and re-layouts: none -> 3.07 us  [the longest x1 1.57 us: per_device(): kunit = lax.dynamic_slice_in_dim(row_kunit, my_start, tokens)]
    dot_general x10 -> x8, matrix products: 9.52 us -> 7.14 us  [dot_first(): lax.dot_general(left, right, (((0,), (0,)), ((), ())), preferred_element_...]
    dot_general x10 -> x8, matrix products: 6.38 us -> 5.02 us  [dot_last(): lax.dot_general(left, right, (((1,), (1,)), ((), ())), preferred_element_...]
where the time goes in v2:
time: 215 us; the launch traced here: 214 us
  Pallas kernels  142 us (66%)
  other arithmetic  32.6 us (15%)
  matrix products  20.2 us (9%)
  local copies, waits for them, and re-layouts  18.1 us (8%)
    pallas_call x1, Pallas kernels, run_tail(): pl.pallas_call(functools.partial(tail_kernel, n_shard, n_ctx, n_tp, early...  70.4 us
    pallas_call x1, Pallas kernels, gather_all(): pl.pallas_call(functools.partial(gather_kernel, n_shard, n_ctx, count), o...  49 us
    pallas_call x3, Pallas kernels, tp_sum(): pl.pallas_call(functools.partial(tp_kernel, n_tp), out_shape=jax.ShapeDty...  22.5 us
    convert_element_type x7, other arithmetic, per_device(): item.astype(jnp.float32)  9.29 us
    dot_general x10, matrix products, dot_plain(): return jnp.dot(left, right, preferred_element_type=jnp.float32)  8.03 us
    dot_general x8, matrix products, dot_first(): lax.dot_general(left, right, (((0,), (0,)), ((), ())), preferred_element_...  7.14 us
    reduce_sum x6, other arithmetic, norm_parts(): scale = lax.rsqrt(jnp.mean(value * value, axis=-1, keepdims=True) + eps)  5.29 us
    dot_general x8, matrix products, dot_last(): lax.dot_general(left, right, (((1,), (1,)), ((), ())), preferred_element_...  5.02 us

profile of v2, /device:TPU:0, one launch (start us, length us, event | category | flops | bytes accessed | tf_op | source)
XLA Modules:
  0.0 214.4 jit_solution(2283716436566929587)
XLA Ops:
  0.7 1.6 pad_maximum_fusion.3.refs_1_
  4.0 1.7 fusion.50
  6.4 49.0 %gather_all.1 = (bf16[640,512]{1,0:T(8,128)(2,1)}, bf16[640,512]{1,0:T(8,128)(2,1)}, bf16[640,512]{1,0:T(8,128)(2,1)}, bf16[640,1024]{1,0:T(8,128)(2,1)}, bf16[6...) custom-call(bf16[160,512]{1,0:T(8,128)(2,1)} %refs_0_.1, ...), custom_call_target="tpu_custom_call" | custom-call | tf_op jit(solution)/shard_map/gather_all/pallas_call | solution.py:203
  57.1 1.9 fusion.11
  60.7 1.9 subtract_convert_fusion
  67.3 8.1 %tp_sum1.1 = f32[128,640]{1,0:T(8,128)} custom-call(bf16[128,640]{1,0:T(8,128)(2,1)} %convolution_convert_fusion.4.part), custom_call_target="tpu_custom_call" | custom-call | tf_op jit(solution)/shard_map/tp_sum1/pallas_call | solution.py:243
  75.4 1.1 multiply_reduce_fusion.9
  76.6 1.7 multiply_reduce_fusion.8
  80.3 1.8 fusion.61
  82.1 1.2 multiply_convert_fusion.3
  84.0 1.2 convolution_convert_fusion.5.part
  85.2 7.3 %tp_sum2.1 = f32[128,640]{1,0:T(8,128)} custom-call(bf16[128,640]{1,0:T(8,128)(2,1)} %convolution_convert_fusion.5.part), custom_call_target="tpu_custom_call" | custom-call | tf_op jit(solution)/shard_map/tp_sum2/pallas_call | solution.py:243
  94.2 1.4 mul.517
  95.5 2.0 multiply_reduce_fusion.1
  97.5 1.9 multiply_convert_fusion.5
  99.5 1.8 multiply_convert_fusion.2
  101.9 1.2 fusion.8.part
  103.1 7.0 %tp_sum3.1 = f32[128,640]{1,0:T(8,128)} custom-call(bf16[128,640]{1,0:T(8,128)(2,1)} %fusion.8.part), custom_call_target="tpu_custom_call" | custom-call | tf_op jit(solution)/shard_map/tp_sum3/pallas_call | solution.py:243
  110.1 1.2 multiply_reduce_fusion.2
  111.4 1.3 multiply_reduce_fusion.3
  112.8 1.2 convolution_convert_fusion.3.refs_0_
  114.0 1.6 convolution_convert_fusion.2.refs_1_
  115.7 1.6 convolution_convert_fusion.1.refs_2_
  117.3 1.6 convolution_convert_fusion.refs_3_
  125.4 1.6 constant_dynamic-slice_fusion.refs_11_
  131.2 70.4 %tail.1 = (bf16[160,512]{1,0:T(8,128)(2,1)}, bf16[160,1024]{1,0:T(8,128)(2,1)}, bf16[160,1024]{1,0:T(8,128)(2,1)}, bf16[160,1024]{1,0:T(8,128)(2,1)}, bf16[160,5...) custom-call(bf16[640,512]{1,0:T(8,128)(2,1)} %convolution_convert_fu, ...), custom_call_target="tpu_custom_call" | custom-call | tf_op jit(solution)/shard_map/tail/pallas_call | solution.py:542
  201.6 1.7 convert_element_type.164
  203.4 1.6 convert_element_type.165
  204.9 1.6 convert_element_type.166
  206.5 1.7 convert_element_type.167
  210.9 1.5 fusion.54
  212.4 1.3 fusion.53
  (224 shorter events, 29.1 us)
Async XLA Ops:
  0.6 5.1 %copy-start.58 = (bf16[160]{0:T(256)(128)(2,1)S(1)}, bf16[160]{0:T(256)(128)(2,1)}, u32[]{:S(2)}) copy-start(bf16[160]{0:T(256)(128)(2,1)} %param.26) | copy-start | bytes 964
  0.7 5.0 %copy-start.59 = (bf16[160]{0:T(256)(128)(2,1)S(1)}, bf16[160]{0:T(256)(128)(2,1)}, u32[]{:S(2)}) copy-start(bf16[160]{0:T(256)(128)(2,1)} %param.27) | copy-start | bytes 964
  0.7 5.0 %copy-start.60 = (bf16[160]{0:T(256)(128)(2,1)S(1)}, bf16[160]{0:T(256)(128)(2,1)}, u32[]{:S(2)}) copy-start(bf16[160]{0:T(256)(128)(2,1)} %param.28) | copy-start | bytes 964
  0.7 5.0 %copy-start.61 = (bf16[160]{0:T(256)(128)(2,1)S(1)}, bf16[160]{0:T(256)(128)(2,1)}, u32[]{:S(2)}) copy-start(bf16[160]{0:T(256)(128)(2,1)} %param.29) | copy-start | bytes 964
  0.7 5.0 %copy-start.62 = (bf16[64]{0:T(256)(128)(2,1)S(1)}, bf16[64]{0:T(256)(128)(2,1)}, u32[]{:S(2)}) copy-start(bf16[64]{0:T(256)(128)(2,1)} %param.30) | copy-start | bytes 388
  0.7 5.0 %copy-start.63 = (bf16[64]{0:T(256)(128)(2,1)S(1)}, bf16[64]{0:T(256)(128)(2,1)}, u32[]{:S(2)}) copy-start(bf16[64]{0:T(256)(128)(2,1)} %param.31) | copy-start | bytes 388
  5.7 118.8 %copy-start.1 = (f32[128,640]{1,0:T(8,128)}, f32[128,640]{1,0:T(8,128)S(1)}, u32[]{:S(2)}) copy-start(f32[128,640]{1,0:T(8,128)S(1)} %get-tuple-element.65.refs_14_) | copy-start | bytes 983044
  59.4 3.1 %copy-start.48 = (f32[512]{0:T(512)}, f32[512]{0:T(512)S(1)}, u32[]{:S(2)}) copy-start(f32[512]{0:T(512)S(1)} %add_rsqrt_fusion) | copy-start | bytes 6148
  59.5 3.1 %copy-start.11 = (bf16[640,512]{1,0:T(8,128)(2,1)S(1)}, bf16[640,512]{1,0:T(8,128)(2,1)}, u32[]{:S(2)}) copy-start(bf16[640,512]{1,0:T(8,128)(2,1)} %get-tuple-element.33.refs_6_) | copy-start | bytes 1966084
  62.5 2.8 %copy-start.36 = (bf16[512,128]{1,0:T(8,128)(2,1)}, bf16[512,128]{1,0:T(8,128)(2,1)S(1)}, u32[]{:S(2)}) copy-start(bf16[512,128]{1,0:T(8,128)(2,1)S(1)} %get-tuple-element.70) | copy-start | bytes 393220
  65.9 9.5 %copy-start.55 = (f32[128]{0:T(128)}, f32[128]{0:T(128)S(1)}, u32[]{:S(2)}) copy-start(f32[128]{0:T(128)S(1)} %log_add_fusion.1) | copy-start | bytes 1540
  66.0 10.6 %copy-start.10 = (f32[128,640]{1,0:T(8,128)S(1)}, f32[128,640]{1,0:T(8,128)}, u32[]{:S(2)}) copy-start(f32[128,640]{1,0:T(8,128)} %param.16) | copy-start | bytes 983044
  66.2 12.0 %copy-start.26 = (bf16[128,256]{1,0:T(8,128)(2,1)}, bf16[128,256]{1,0:T(8,128)(2,1)S(1)}, u32[]{:S(2)}) copy-start(bf16[128,256]{1,0:T(8,128)(2,1)S(1)} %convolution_convert_fusion.8) | copy-start | bytes 196612
  78.3 3.8 %copy-start.2 = (bf16[640,1024]{1,0:T(8,128)(2,1)S(1)}, bf16[640,1024]{1,0:T(8,128)(2,1)}, u32[]{:S(2)}) copy-start(bf16[640,1024]{1,0:T(8,128)(2,1)} %get-tuple-element.38) | copy-start | bytes 3932164
  80.3 3.0 %copy-start.6 = (bf16[128,640]{1,0:T(8,128)(2,1)}, bf16[128,640]{1,0:T(8,128)(2,1)S(1)}, u32[]{:S(2)}) copy-start(bf16[128,640]{1,0:T(8,128)(2,1)S(1)} %multiply_convert_fusion.6) | copy-start | bytes 491524
  95.5 4.0 %copy-start.17 = (f32[128,1024]{1,0:T(8,128)S(1)}, f32[128,1024]{1,0:T(8,128)}, u32[]{:S(2)}) copy-start(f32[128,1024]{1,0:T(8,128)} %copy-done.16) | copy-start | bytes 1572868
  95.5 4.0 %copy-start.19 = (bf16[640,1024]{1,0:T(8,128)(2,1)S(1)}, bf16[640,1024]{1,0:T(8,128)(2,1)}, u32[]{:S(2)}) copy-start(bf16[640,1024]{1,0:T(8,128)(2,1)} %get-tuple-element.39) | copy-start | bytes 3932164
  101.8 8.3 %copy-start.52 = (f32[128]{0:T(128)S(1)}, f32[128]{0:T(128)}, u32[]{:S(2)}) copy-start(f32[128]{0:T(128)} %copy-done.51) | copy-start | bytes 1540
  101.8 9.5 %copy-start = (f32[128,640]{1,0:T(8,128)S(1)}, f32[128,640]{1,0:T(8,128)}, u32[]{:S(2)}) copy-start(f32[128,640]{1,0:T(8,128)} %tp_sum1.1) | copy-start | bytes 983044
  101.8 9.5 %copy-start.9 = (f32[128,640]{1,0:T(8,128)S(1)}, f32[128,640]{1,0:T(8,128)}, u32[]{:S(2)}) copy-start(f32[128,640]{1,0:T(8,128)} %param.17) | copy-start | bytes 983044
  101.8 9.5 %copy-start.50 = (f32[128]{0:T(128)S(1)}, f32[128]{0:T(128)}, u32[]{:S(2)}) copy-start(f32[128]{0:T(128)} %copy-done.49) | copy-start | bytes 1540
  111.4 2.7 %copy-start.7 = (bf16[128,640]{1,0:T(8,128)(2,1)S(1)}, bf16[128,640]{1,0:T(8,128)(2,1)}, u32[]{:S(2)}) copy-start(bf16[128,640]{1,0:T(8,128)(2,1)} %copy-done.6) | copy-start | bytes 491524
  112.7 3.0 %copy-start.8 = (f32[128,640]{1,0:T(8,128)}, f32[128,640]{1,0:T(8,128)S(1)}, u32[]{:S(2)}) copy-start(f32[128,640]{1,0:T(8,128)S(1)} %get-tuple-element.59.refs_17_) | copy-start | bytes 983044
  114.0 3.2 %copy-start.15 = (bf16[128,1024]{1,0:T(8,128)(2,1)S(1)}, bf16[128,1024]{1,0:T(8,128)(2,1)}, u32[]{:S(2)}) copy-start(bf16[128,1024]{1,0:T(8,128)(2,1)} %copy-done.14) | copy-start | bytes 786436
  115.7 3.2 %copy-start.13 = (bf16[640,512]{1,0:T(8,128)(2,1)S(1)}, bf16[640,512]{1,0:T(8,128)(2,1)}, u32[]{:S(2)}) copy-start(bf16[640,512]{1,0:T(8,128)(2,1)} %get-tuple-element.36) | copy-start | bytes 1966084
  123.7 4.8 %copy-start.41 = (f32[4,64]{1,0:T(4,128)S(1)}, f32[4,64]{1,0:T(4,128)}, u32[]{:S(2)}) copy-start(f32[4,64]{1,0:T(4,128)} %copy-done.40) | copy-start | bytes 3076
  123.7 5.4 %copy-start.57 = (f32[128,1]{0,1:T(1,128)S(1)}, f32[128,1]{0,1:T(1,128)}, u32[]{:S(2)}) copy-start(f32[128,1]{0,1:T(1,128)} %get-tuple-element.94) | copy-start | bytes 1540
  123.7 6.8 %copy-start.46 = (f32[640]{0:T(1024)S(1)}, f32[640]{0:T(1024)}, u32[]{:S(2)}) copy-start(f32[640]{0:T(1024)} %get-tuple-element.49) | copy-start | bytes 7684
  201.6 6.6 %copy-start.35 = (bf16[160,1024]{1,0:T(8,128)(2,1)S(1)}, bf16[160,1024]{1,0:T(8,128)(2,1)}, u32[]{:S(2)}) copy-start(bf16[160,1024]{1,0:T(8,128)(2,1)} %get-tuple-element.45) | copy-start | bytes 983044
  201.6 7.5 %copy-start.34 = (bf16[160,1024]{1,0:T(8,128)(2,1)S(1)}, bf16[160,1024]{1,0:T(8,128)(2,1)}, u32[]{:S(2)}) copy-start(bf16[160,1024]{1,0:T(8,128)(2,1)} %get-tuple-element.46) | copy-start | bytes 983044
  204.9 5.1 %copy-start.33 = (bf16[160,1024]{1,0:T(8,128)(2,1)S(1)}, bf16[160,1024]{1,0:T(8,128)(2,1)}, u32[]{:S(2)}) copy-start(bf16[160,1024]{1,0:T(8,128)(2,1)} %get-tuple-element.47) | copy-start | bytes 983044
  208.2 5.4 %copy-start.32 = (f32[128,640]{1,0:T(8,128)S(1)}, f32[128,640]{1,0:T(8,128)}, u32[]{:S(2)}) copy-start(f32[128,640]{1,0:T(8,128)} %get-tuple-element.120) | copy-start | bytes 983044
  (33 other events, 43.1 us)

commit v3 on v2

--- a/solution.py
+++ b/solution.py
@@ -175,6 +175,15 @@
     for item in own:
         item.start()
     across = {}
+    other = lax.rem(far, WAYS)
+
+    def relay(d):
+        source = lax.rem(shard - d + n_shard, n_shard)
+        for a in range(count):
+            across[d, a].wait_recv()
+            block = outs[a].at[block_rows(source, rows), columns(other, widths[a])]
+            started.append(send(block, block, sems_c, (d - 1, a), (shard, near, tp)))
+
     for d in range(1, n_shard):
         source = lax.rem(shard - d + n_shard, n_shard)
         for a in range(count):
@@ -182,13 +191,9 @@
             block = outs[a].at[block_rows(source, rows), columns(member, widths[a])]
             across[d, a] = send(block, block, sems_f, (d - 1, a), (shard, far, tp))
             started.append(send(block, block, sems_n, (d - 1, a), (shard, near, tp)))
-    other = lax.rem(far, WAYS)
-    for d in range(1, n_shard):
-        source = lax.rem(shard - d + n_shard, n_shard)
-        for a in range(count):
-            across[d, a].wait_recv()
-            block = outs[a].at[block_rows(source, rows), columns(other, widths[a])]
-            started.append(send(block, block, sems_c, (d - 1, a), (shard, near, tp)))
+        if d > 1:
+            relay(d - 1)
+    relay(n_shard - 1)
     for item in started:
         item.wait()
     for item in list(first.values()) + list(across.values()):
@@ -317,21 +322,22 @@
 
     def start_core(batch):
         for slot, quarter in ((1, opposite), (0, beside)):
-            for a in batches[batch]:
-                core[slot, a] = send(
-                    grads[a].at[:, columns(quarter, widths[a])],
-                    half.at[slot, :, pl.ds(starts[a], widths[a])],
-                    s_core,
-                    (slot, a),
-                    near_id,
-                )
+            for d in order:
+                where = block_rows(targets[d], rows)
+                for a in batches[batch]:
+                    core[slot, a, d] = send(
+                        grads[a].at[where, columns(quarter, widths[a])],
+                        half.at[slot, where, pl.ds(starts[a], widths[a])],
+                        s_core,
+                        (slot, a, d),
+                        near_id,
+                    )
 
     def start_over(batch):
-        for a in batches[batch]:
-            core[1, a].wait_recv()
         for d in order:
             where = block_rows(targets[d], rows)
             for a in batches[batch]:
+                core[1, a, d].wait_recv()
                 cols = pl.ds(starts[a], widths[a])
                 total = half[1, where, cols].astype(jnp.float32) + grads[a][
                     where, columns(other, widths[a])
@@ -346,12 +352,11 @@
             )
 
     def start_along(batch):
-        for a in batches[batch]:
-            core[0, a].wait_recv()
         for d in order:
             where = block_rows(targets[d], rows)
             over[batch, d].wait_recv()
             for a in batches[batch]:
+                core[0, a, d].wait_recv()
                 cols = pl.ds(starts[a], widths[a])
                 total = (
                     half[0, where, cols].astype(jnp.float32)
@@ -413,6 +418,7 @@
     ]
     start_core(0)
     late_q[...] = dot_plain(xn1_t[...], dqp[...]).astype(jnp.bfloat16)
+    start_over(0)
     dxn1 = dot_last(dqp[...], qw[...])
     dkv = terms[block_rows(ctx, tokens), :].astype(jnp.float32)
     for d in range(1, n_ctx):
@@ -427,7 +433,6 @@
         send(part, part_in.at[d - 1], s_part, d - 1, t_ids[d - 1]) for d in range(1, n_tp)
     ]
     late_kv[...] = dot_plain(xn1_t[...], dkvp).astype(jnp.bfloat16)
-    start_over(0)
     start_core(1)
     dxn1 = part[...].astype(jnp.float32)
     for d in range(1, n_tp):
@@ -568,7 +573,7 @@
             pltpu.VMEM((n_groups,) + gain.shape, full),
             pltpu.VMEM((n_tp,) + gain.shape, full),
         ]
-        + dma(2, count)
+        + dma(2, count, n_shard)
         + dma(2, n_shard)
         + dma(2, n_shard - 1)
         + dma(2, max(n_groups - 1, 1))

time: 215 us -> 215 us (level)
  no operation moved by 1% of the time
where the time goes in v3:
time: 215 us; the launch traced here: 214 us
  Pallas kernels  141 us (66%)
  other arithmetic  32.6 us (15%)
  matrix products  20.2 us (9%)
  local copies, waits for them, and re-layouts  18.1 us (8%)
    pallas_call x1, Pallas kernels, run_tail(): pl.pallas_call(functools.partial(tail_kernel, n_shard, n_ctx, n_tp, early...  69.8 us
    pallas_call x1, Pallas kernels, gather_all(): pl.pallas_call(functools.partial(gather_kernel, n_shard, n_ctx, count), o...  49 us
    pallas_call x3, Pallas kernels, tp_sum(): pl.pallas_call(functools.partial(tp_kernel, n_tp), out_shape=jax.ShapeDty...  22.5 us
    convert_element_type x7, other arithmetic, per_device(): item.astype(jnp.float32)  9.29 us
    dot_general x10, matrix products, dot_plain(): return jnp.dot(left, right, preferred_element_type=jnp.float32)  8.03 us
    dot_general x8, matrix products, dot_first(): lax.dot_general(left, right, (((0,), (0,)), ((), ())), preferred_element_...  7.14 us
    reduce_sum x6, other arithmetic, norm_parts(): scale = lax.rsqrt(jnp.mean(value * value, axis=-1, keepdims=True) + eps)  5.29 us
    dot_general x8, matrix products, dot_last(): lax.dot_general(left, right, (((1,), (1,)), ((), ())), preferred_element_...  5.02 us

profile of v3, /device:TPU:0, one launch (start us, length us, event | category | flops | bytes accessed | tf_op | source)
XLA Modules:
  0.0 213.7 jit_solution(475261992292772529)
XLA Ops:
  0.7 1.6 pad_maximum_fusion.3.refs_1_
  4.0 1.7 fusion.50
  6.4 49.0 %gather_all.1 = (bf16[640,512]{1,0:T(8,128)(2,1)}, bf16[640,512]{1,0:T(8,128)(2,1)}, bf16[640,512]{1,0:T(8,128)(2,1)}, bf16[640,1024]{1,0:T(8,128)(2,1)}, bf16[6...) custom-call(bf16[160,512]{1,0:T(8,128)(2,1)} %refs_0_.1, ...), custom_call_target="tpu_custom_call" | custom-call | tf_op jit(solution)/shard_map/gather_all/pallas_call | solution.py:208
  57.1 1.9 fusion.11
  60.7 1.9 subtract_convert_fusion
  67.3 8.1 %tp_sum1.1 = f32[128,640]{1,0:T(8,128)} custom-call(bf16[128,640]{1,0:T(8,128)(2,1)} %convolution_convert_fusion.4.part), custom_call_target="tpu_custom_call" | custom-call | tf_op jit(solution)/shard_map/tp_sum1/pallas_call | solution.py:248
  75.4 1.1 multiply_reduce_fusion.9
  76.6 1.7 multiply_reduce_fusion.8
  80.3 1.8 fusion.61
  82.1 1.2 multiply_convert_fusion.3
  84.0 1.2 convolution_convert_fusion.5.part
  85.2 7.3 %tp_sum2.1 = f32[128,640]{1,0:T(8,128)} custom-call(bf16[128,640]{1,0:T(8,128)(2,1)} %convolution_convert_fusion.5.part), custom_call_target="tpu_custom_call" | custom-call | tf_op jit(solution)/shard_map/tp_sum2/pallas_call | solution.py:248
  94.2 1.4 mul.517
  95.5 2.0 multiply_reduce_fusion.1
  97.5 1.9 multiply_convert_fusion.5
  99.5 1.8 multiply_convert_fusion.2
  101.9 1.2 fusion.8.part
  103.1 7.0 %tp_sum3.1 = f32[128,640]{1,0:T(8,128)} custom-call(bf16[128,640]{1,0:T(8,128)(2,1)} %fusion.8.part), custom_call_target="tpu_custom_call" | custom-call | tf_op jit(solution)/shard_map/tp_sum3/pallas_call | solution.py:248
  110.1 1.2 multiply_reduce_fusion.2
  111.4 1.3 multiply_reduce_fusion.3
  112.8 1.2 convolution_convert_fusion.3.refs_0_
  114.0 1.6 convolution_convert_fusion.2.refs_1_
  115.7 1.6 convolution_convert_fusion.1.refs_2_
  117.3 1.6 convolution_convert_fusion.refs_3_
  125.4 1.6 constant_dynamic-slice_fusion.refs_11_
  131.2 69.8 %tail.1 = (bf16[160,512]{1,0:T(8,128)(2,1)}, bf16[160,1024]{1,0:T(8,128)(2,1)}, bf16[160,1024]{1,0:T(8,128)(2,1)}, bf16[160,1024]{1,0:T(8,128)(2,1)}, bf16[160,5...) custom-call(bf16[640,512]{1,0:T(8,128)(2,1)} %convolution_convert_fu, ...), custom_call_target="tpu_custom_call" | custom-call | tf_op jit(solution)/shard_map/tail/pallas_call | solution.py:547
  201.0 1.7 convert_element_type.164
  202.7 1.6 convert_element_type.165
  204.3 1.6 convert_element_type.166
  205.9 1.7 convert_element_type.167
  210.3 1.5 fusion.54
  211.7 1.3 fusion.53
  (224 shorter events, 29.1 us)
Async XLA Ops:
  0.6 5.1 %copy-start.58 = (bf16[160]{0:T(256)(128)(2,1)S(1)}, bf16[160]{0:T(256)(128)(2,1)}, u32[]{:S(2)}) copy-start(bf16[160]{0:T(256)(128)(2,1)} %param.26) | copy-start | bytes 964
  0.7 5.0 %copy-start.59 = (bf16[160]{0:T(256)(128)(2,1)S(1)}, bf16[160]{0:T(256)(128)(2,1)}, u32[]{:S(2)}) copy-start(bf16[160]{0:T(256)(128)(2,1)} %param.27) | copy-start | bytes 964
  0.7 5.0 %copy-start.60 = (bf16[160]{0:T(256)(128)(2,1)S(1)}, bf16[160]{0:T(256)(128)(2,1)}, u32[]{:S(2)}) copy-start(bf16[160]{0:T(256)(128)(2,1)} %param.28) | copy-start | bytes 964
  0.7 5.0 %copy-start.61 = (bf16[160]{0:T(256)(128)(2,1)S(1)}, bf16[160]{0:T(256)(128)(2,1)}, u32[]{:S(2)}) copy-start(bf16[160]{0:T(256)(128)(2,1)} %param.29) | copy-start | bytes 964
  0.7 5.0 %copy-start.62 = (bf16[64]{0:T(256)(128)(2,1)S(1)}, bf16[64]{0:T(256)(128)(2,1)}, u32[]{:S(2)}) copy-start(bf16[64]{0:T(256)(128)(2,1)} %param.30) | copy-start | bytes 388
  0.7 5.0 %copy-start.63 = (bf16[64]{0:T(256)(128)(2,1)S(1)}, bf16[64]{0:T(256)(128)(2,1)}, u32[]{:S(2)}) copy-start(bf16[64]{0:T(256)(128)(2,1)} %param.31) | copy-start | bytes 388
  5.7 118.8 %copy-start.1 = (f32[128,640]{1,0:T(8,128)}, f32[128,640]{1,0:T(8,128)S(1)}, u32[]{:S(2)}) copy-start(f32[128,640]{1,0:T(8,128)S(1)} %get-tuple-element.65.refs_14_) | copy-start | bytes 983044
  59.4 3.1 %copy-start.48 = (f32[512]{0:T(512)}, f32[512]{0:T(512)S(1)}, u32[]{:S(2)}) copy-start(f32[512]{0:T(512)S(1)} %add_rsqrt_fusion) | copy-start | bytes 6148
  59.5 3.1 %copy-start.11 = (bf16[640,512]{1,0:T(8,128)(2,1)S(1)}, bf16[640,512]{1,0:T(8,128)(2,1)}, u32[]{:S(2)}) copy-start(bf16[640,512]{1,0:T(8,128)(2,1)} %get-tuple-element.33.refs_6_) | copy-start | bytes 1966084
  62.5 2.8 %copy-start.36 = (bf16[512,128]{1,0:T(8,128)(2,1)}, bf16[512,128]{1,0:T(8,128)(2,1)S(1)}, u32[]{:S(2)}) copy-start(bf16[512,128]{1,0:T(8,128)(2,1)S(1)} %get-tuple-element.70) | copy-start | bytes 393220
  65.9 9.5 %copy-start.55 = (f32[128]{0:T(128)}, f32[128]{0:T(128)S(1)}, u32[]{:S(2)}) copy-start(f32[128]{0:T(128)S(1)} %log_add_fusion.1) | copy-start | bytes 1540
  66.0 10.6 %copy-start.10 = (f32[128,640]{1,0:T(8,128)S(1)}, f32[128,640]{1,0:T(8,128)}, u32[]{:S(2)}) copy-start(f32[128,640]{1,0:T(8,128)} %param.16) | copy-start | bytes 983044
  66.2 12.0 %copy-start.26 = (bf16[128,256]{1,0:T(8,128)(2,1)}, bf16[128,256]{1,0:T(8,128)(2,1)S(1)}, u32[]{:S(2)}) copy-start(bf16[128,256]{1,0:T(8,128)(2,1)S(1)} %convolution_convert_fusion.8) | copy-start | bytes 196612
  78.3 3.8 %copy-start.2 = (bf16[640,1024]{1,0:T(8,128)(2,1)S(1)}, bf16[640,1024]{1,0:T(8,128)(2,1)}, u32[]{:S(2)}) copy-start(bf16[640,1024]{1,0:T(8,128)(2,1)} %get-tuple-element.38) | copy-start | bytes 3932164
  80.3 3.0 %copy-start.6 = (bf16[128,640]{1,0:T(8,128)(2,1)}, bf16[128,640]{1,0:T(8,128)(2,1)S(1)}, u32[]{:S(2)}) copy-start(bf16[128,640]{1,0:T(8,128)(2,1)S(1)} %multiply_convert_fusion.6) | copy-start | bytes 491524
  95.5 4.0 %copy-start.17 = (f32[128,1024]{1,0:T(8,128)S(1)}, f32[128,1024]{1,0:T(8,128)}, u32[]{:S(2)}) copy-start(f32[128,1024]{1,0:T(8,128)} %copy-done.16) | copy-start | bytes 1572868
  95.5 4.0 %copy-start.19 = (bf16[640,1024]{1,0:T(8,128)(2,1)S(1)}, bf16[640,1024]{1,0:T(8,128)(2,1)}, u32[]{:S(2)}) copy-start(bf16[640,1024]{1,0:T(8,128)(2,1)} %get-tuple-element.39) | copy-start | bytes 3932164
  101.8 8.3 %copy-start.52 = (f32[128]{0:T(128)S(1)}, f32[128]{0:T(128)}, u32[]{:S(2)}) copy-start(f32[128]{0:T(128)} %copy-done.51) | copy-start | bytes 1540
  101.8 9.5 %copy-start = (f32[128,640]{1,0:T(8,128)S(1)}, f32[128,640]{1,0:T(8,128)}, u32[]{:S(2)}) copy-start(f32[128,640]{1,0:T(8,128)} %tp_sum1.1) | copy-start | bytes 983044
  101.8 9.5 %copy-start.9 = (f32[128,640]{1,0:T(8,128)S(1)}, f32[128,640]{1,0:T(8,128)}, u32[]{:S(2)}) copy-start(f32[128,640]{1,0:T(8,128)} %param.17) | copy-start | bytes 983044
  101.8 9.5 %copy-start.50 = (f32[128]{0:T(128)S(1)}, f32[128]{0:T(128)}, u32[]{:S(2)}) copy-start(f32[128]{0:T(128)} %copy-done.49) | copy-start | bytes 1540
  111.4 2.7 %copy-start.7 = (bf16[128,640]{1,0:T(8,128)(2,1)S(1)}, bf16[128,640]{1,0:T(8,128)(2,1)}, u32[]{:S(2)}) copy-start(bf16[128,640]{1,0:T(8,128)(2,1)} %copy-done.6) | copy-start | bytes 491524
  112.7 3.0 %copy-start.8 = (f32[128,640]{1,0:T(8,128)}, f32[128,640]{1,0:T(8,128)S(1)}, u32[]{:S(2)}) copy-start(f32[128,640]{1,0:T(8,128)S(1)} %get-tuple-element.59.refs_17_) | copy-start | bytes 983044
  114.0 3.2 %copy-start.15 = (bf16[128,1024]{1,0:T(8,128)(2,1)S(1)}, bf16[128,1024]{1,0:T(8,128)(2,1)}, u32[]{:S(2)}) copy-start(bf16[128,1024]{1,0:T(8,128)(2,1)} %copy-done.14) | copy-start | bytes 786436
  115.7 3.2 %copy-start.13 = (bf16[640,512]{1,0:T(8,128)(2,1)S(1)}, bf16[640,512]{1,0:T(8,128)(2,1)}, u32[]{:S(2)}) copy-start(bf16[640,512]{1,0:T(8,128)(2,1)} %get-tuple-element.36) | copy-start | bytes 1966084
  123.7 4.8 %copy-start.41 = (f32[4,64]{1,0:T(4,128)S(1)}, f32[4,64]{1,0:T(4,128)}, u32[]{:S(2)}) copy-start(f32[4,64]{1,0:T(4,128)} %copy-done.40) | copy-start | bytes 3076
  123.7 5.4 %copy-start.57 = (f32[128,1]{0,1:T(1,128)S(1)}, f32[128,1]{0,1:T(1,128)}, u32[]{:S(2)}) copy-start(f32[128,1]{0,1:T(1,128)} %get-tuple-element.94) | copy-start | bytes 1540
  123.7 6.8 %copy-start.46 = (f32[640]{0:T(1024)S(1)}, f32[640]{0:T(1024)}, u32[]{:S(2)}) copy-start(f32[640]{0:T(1024)} %get-tuple-element.49) | copy-start | bytes 7684
  200.9 6.6 %copy-start.35 = (bf16[160,1024]{1,0:T(8,128)(2,1)S(1)}, bf16[160,1024]{1,0:T(8,128)(2,1)}, u32[]{:S(2)}) copy-start(bf16[160,1024]{1,0:T(8,128)(2,1)} %get-tuple-element.45) | copy-start | bytes 983044
  200.9 7.5 %copy-start.34 = (bf16[160,1024]{1,0:T(8,128)(2,1)S(1)}, bf16[160,1024]{1,0:T(8,128)(2,1)}, u32[]{:S(2)}) copy-start(bf16[160,1024]{1,0:T(8,128)(2,1)} %get-tuple-element.46) | copy-start | bytes 983044
  204.3 5.1 %copy-start.33 = (bf16[160,1024]{1,0:T(8,128)(2,1)S(1)}, bf16[160,1024]{1,0:T(8,128)(2,1)}, u32[]{:S(2)}) copy-start(bf16[160,1024]{1,0:T(8,128)(2,1)} %get-tuple-element.47) | copy-start | bytes 983044
  207.5 5.4 %copy-start.32 = (f32[128,640]{1,0:T(8,128)S(1)}, f32[128,640]{1,0:T(8,128)}, u32[]{:S(2)}) copy-start(f32[128,640]{1,0:T(8,128)} %get-tuple-element.120) | copy-start | bytes 983044
  (33 other events, 43.1 us)
